TPU v7x, 32 devices: a whole 2x2x4 slice. The times are simulated.
32 devices in a mesh: dp: 8 (over y, x, core), mp: 4 (over z).
Axes of the slice: x: 2, y: 2, z: 4, core: 2. Of those that a mesh axis runs over, the one named last changes fastest.
Arguments:
- latent: bfloat16 [8192, 1152], P('dp'), may hold values from -6 to 6
- condition: bfloat16 [8, 1152], P('dp'), may hold values from -6 to 6
- lengths: int32 [8], P('dp'), may hold values from 128 to 1024, as said below
- w_ada: bfloat16 [1152, 6912], P(None, 'mp'), may hold values from -0.1875 to 0.1875
- b_ada: bfloat16 [6912], P('mp'), may hold values from -3 to 3
- w_qkv: bfloat16 [1152, 3, 1152], P(None, None, 'mp'), may hold values from -0.1875 to 0.1875
- b_qv: bfloat16 [2, 1152], P(None, 'mp'), may hold values from -3 to 3
- w_out: bfloat16 [1152, 1152], P('mp'), may hold values from -0.75 to 0.75
- b_out: bfloat16 [1152], replicated, may hold values from -2 to 2
- w_fc1: bfloat16 [1152, 4608], P(None, 'mp'), may hold values from -0.1875 to 0.1875
- b_fc1: bfloat16 [4608], P('mp'), may hold values from -2 to 2
- w_fc2: bfloat16 [4608, 1152], P('mp'), may hold values from -0.09375 to 0.09375
- b_fc2: bfloat16 [1152], replicated, may hold values from -2 to 2
- cotangent: bfloat16 [8192, 1152], P('dp'), may hold values from -6 to 6
Outputs:
- output: bfloat16 [8192, 1152], P('dp')
- grad_latent: bfloat16 [8192, 1152], P('dp')
- grad_condition: float32 [8, 1152], P('dp')
- grad_w_ada: float32 [1152, 6912], P(None, 'mp')
- grad_b_ada: float32 [6912], P('mp')
- grad_w_qkv: float32 [1152, 3, 1152], P(None, None, 'mp')
- grad_b_qv: float32 [2, 1152], P(None, 'mp')
- grad_w_out: float32 [1152, 1152], P('mp')
- grad_b_out: float32 [1152], replicated
- grad_w_fc1: float32 [1152, 4608], P(None, 'mp')
- grad_b_fc1: float32 [4608], P('mp')
- grad_w_fc2: float32 [4608, 1152], P('mp')
- grad_b_fc2: float32 [1152], replicated
Inputs may be any that keep to these rules, and one draw needn't show every extreme that they name: The first lengths[s] of sample s's 1024 rows are real tokens, the rest padding; some sample has all 1024 rows real.
All inputs are finite; a program needn't handle non-finite values.
Results may differ from a plain program's by a relative error of at most 0.02.
The roundings to bfloat16 on the way count: a program that leaves them out, or rounds other values in their place, can miss the bound.
Values may be sent and summed in bfloat16 or wider, within the bound.
No kernel may reach another device: no remote copies, remote signals or barrier semaphores. Data moves between devices by JAX's collectives and lax.ppermute only.
A program may use at most 192 MiB of HBM per device.

v0:
```python
import math

import jax
import jax.numpy as jnp
from jax import lax
from jax.sharding import PartitionSpec as P

HD = 72


PRECISE = lax.Precision.HIGHEST
EPSILON = 1e-06


def layer_norm(values):
    row_mean = jnp.mean(values, axis=-1, keepdims=True)
    centred = values - row_mean
    row_var = jnp.mean(centred * centred, axis=-1, keepdims=True)
    return centred * lax.rsqrt(row_var + EPSILON)


def modulate(values, scale_tok, shift_tok):
    return layer_norm(values) * (1.0 + scale_tok) + shift_tok


def gelu_tanh(values):
    return jax.nn.gelu(values, approximate=True)


def masked_scores(query_heads, key_heads, real_count):
    seq_len = query_heads.shape[0]
    scores = jnp.einsum(
        "qhd,khd->hqk", query_heads, key_heads, preferred_element_type=jnp.float32
    ) * (1.0 / math.sqrt(HD))
    is_valid = jnp.arange(seq_len, dtype=jnp.int32) < real_count
    return jnp.where(is_valid[None, None, :], scores, -1e30)


def attend_forward(packed):
    query_rows, key_rows, value_rows, real_count = packed
    seq_len, group_width = query_rows.shape
    head_count = group_width // HD
    query_heads = query_rows.reshape(seq_len, head_count, HD)
    key_heads = key_rows.reshape(seq_len, head_count, HD)
    value_heads = value_rows.reshape(seq_len, head_count, HD)
    scores = masked_scores(query_heads, key_heads, real_count)
    row_max = jnp.max(scores, axis=-1, keepdims=True)
    exponent = jnp.exp(scores - row_max)
    row_total = jnp.sum(exponent, axis=-1, keepdims=True)
    low_probs = (exponent / row_total).astype(jnp.bfloat16)
    mixed = jnp.einsum("hqk,khd->qhd", low_probs, value_heads, preferred_element_type=jnp.float32)
    logsum = (row_max + jnp.log(row_total))[..., 0]
    return (mixed.astype(jnp.bfloat16).reshape(seq_len, group_width), logsum)


def attend_backward(packed):
    query_rows, key_rows, value_rows, grad_rows, logsum, real_count = packed
    seq_len, group_width = query_rows.shape
    head_count = group_width // HD
    query_heads = query_rows.reshape(seq_len, head_count, HD)
    key_heads = key_rows.reshape(seq_len, head_count, HD)
    value_heads = value_rows.reshape(seq_len, head_count, HD)
    grad_heads = grad_rows.reshape(seq_len, head_count, HD)
    scores = masked_scores(query_heads, key_heads, real_count)
    probability = jnp.exp(scores - logsum[..., None])
    low_probs = probability.astype(jnp.bfloat16)
    grad_value = jnp.einsum(
        "hqk,qhd->khd", low_probs, grad_heads, preferred_element_type=jnp.float32
    )
    grad_probs = jnp.einsum(
        "qhd,khd->hqk", grad_heads, value_heads, preferred_element_type=jnp.float32
    )
    row_inner = jnp.sum(probability * grad_probs, axis=-1, keepdims=True)
    grad_scores = (probability * (grad_probs - row_inner)).astype(jnp.bfloat16)
    scaling = 1.0 / math.sqrt(HD)
    grad_query = (
        jnp.einsum("hqk,khd->qhd", grad_scores, key_heads, preferred_element_type=jnp.float32)
        * scaling
    )
    grad_key = (
        jnp.einsum("hqk,qhd->khd", grad_scores, query_heads, preferred_element_type=jnp.float32)
        * scaling
    )
    shape_out = (seq_len, group_width)
    return (
        grad_query.astype(jnp.bfloat16).reshape(shape_out),
        grad_key.astype(jnp.bfloat16).reshape(shape_out),
        grad_value.astype(jnp.bfloat16).reshape(shape_out),
    )


def local(
    latent,
    condition,
    lengths,
    w_ada,
    b_ada,
    w_qkv,
    b_qv,
    w_out,
    b_out,
    w_fc1,
    b_fc1,
    w_fc2,
    b_fc2,
    cotangent,
):
    samples = condition.shape[0]
    tokens, width_model = latent.shape
    seq_len = tokens // samples
    group_width = w_qkv.shape[2]
    silu_cond = jax.nn.silu(condition.astype(jnp.float32))
    ada_weight = w_ada.astype(jnp.float32)
    mod_part = jnp.dot(silu_cond, ada_weight, precision=PRECISE) + b_ada.astype(jnp.float32)
    modulation = lax.all_gather(mod_part, "mp", axis=1, tiled=True).reshape(
        samples, 6, 1, width_model
    )
    shift_one = modulation[:, 0]
    scale_one = modulation[:, 1]
    gate_one = modulation[:, 2]
    shift_two = modulation[:, 3]
    scale_two = modulation[:, 4]
    gate_two = modulation[:, 5]
    inputs = latent.astype(jnp.float32).reshape(samples, seq_len, width_model)
    normed_one = (
        modulate(inputs, scale_one, shift_one).astype(jnp.bfloat16).reshape(tokens, width_model)
    )
    qkv_weight = w_qkv.reshape(width_model, 3 * group_width)
    projected = jnp.dot(normed_one, qkv_weight, preferred_element_type=jnp.float32)
    query = (projected[:, :group_width] + b_qv[0].astype(jnp.float32)).astype(jnp.bfloat16)
    key_rows = projected[:, group_width : 2 * group_width].astype(jnp.bfloat16)
    value_rows = (projected[:, 2 * group_width :] + b_qv[1].astype(jnp.float32)).astype(
        jnp.bfloat16
    )
    query_s = query.reshape(samples, seq_len, group_width)
    key_s = key_rows.reshape(samples, seq_len, group_width)
    value_s = value_rows.reshape(samples, seq_len, group_width)
    attended, logsums = lax.map(attend_forward, (query_s, key_s, value_s, lengths))
    attended = attended.reshape(tokens, group_width)
    attn_term = jnp.dot(attended, w_out, preferred_element_type=jnp.float32)
    attn_branch = lax.psum(attn_term.astype(jnp.bfloat16), "mp").astype(jnp.float32) + b_out.astype(
        jnp.float32
    )
    attn_three = attn_branch.reshape(samples, seq_len, width_model)
    middle = inputs + gate_one * attn_three
    normed_two = (
        modulate(middle, scale_two, shift_two).astype(jnp.bfloat16).reshape(tokens, width_model)
    )
    hidden_pre = jnp.dot(normed_two, w_fc1, preferred_element_type=jnp.float32) + b_fc1.astype(
        jnp.float32
    )
    gelu_value, gelu_back = jax.vjp(gelu_tanh, hidden_pre)
    activated = gelu_value.astype(jnp.bfloat16)
    mlp_term = jnp.dot(activated, w_fc2, preferred_element_type=jnp.float32)
    mlp_branch = lax.psum(mlp_term.astype(jnp.bfloat16), "mp").astype(jnp.float32) + b_fc2.astype(
        jnp.float32
    )
    mlp_three = mlp_branch.reshape(samples, seq_len, width_model)
    output = (middle + gate_two * mlp_three).reshape(tokens, width_model).astype(jnp.bfloat16)
    grad_out = cotangent.astype(jnp.float32).reshape(samples, seq_len, width_model)
    grad_gate_two = jnp.sum(grad_out * mlp_three, axis=1, keepdims=True)
    grad_mlp = (gate_two * grad_out).astype(jnp.bfloat16).reshape(tokens, width_model)
    grad_fc2 = jnp.einsum("ti,td->id", activated, grad_mlp, preferred_element_type=jnp.float32)
    grad_bias_fc2 = jnp.sum(grad_mlp.astype(jnp.float32), axis=0)
    grad_activated = jnp.einsum("td,id->ti", grad_mlp, w_fc2, preferred_element_type=jnp.float32)
    grad_hidden = gelu_back(grad_activated)[0].astype(jnp.bfloat16)
    grad_fc1 = jnp.einsum("td,ti->di", normed_two, grad_hidden, preferred_element_type=jnp.float32)
    grad_bias_fc1 = jnp.sum(grad_hidden.astype(jnp.float32), axis=0)
    normed_two_term = jnp.einsum(
        "ti,di->td", grad_hidden, w_fc1, preferred_element_type=jnp.float32
    )
    grad_normed_two = lax.psum(normed_two_term.astype(jnp.bfloat16), "mp").astype(jnp.float32)
    _, second_back = jax.vjp(modulate, middle, scale_two, shift_two)
    middle_norm, grad_scale_two, grad_shift_two = second_back(
        grad_normed_two.reshape(samples, seq_len, width_model)
    )
    grad_middle = grad_out + middle_norm
    grad_gate_one = jnp.sum(grad_middle * attn_three, axis=1, keepdims=True)
    grad_attn = (gate_one * grad_middle).astype(jnp.bfloat16).reshape(tokens, width_model)
    grad_out_proj = jnp.einsum("tf,td->fd", attended, grad_attn, preferred_element_type=jnp.float32)
    grad_bias_out = jnp.sum(grad_attn.astype(jnp.float32), axis=0)
    grad_attended = jnp.einsum(
        "td,fd->tf", grad_attn, w_out, preferred_element_type=jnp.float32
    ).astype(jnp.bfloat16)
    grad_query, grad_key, grad_value = lax.map(
        attend_backward,
        (
            query_s,
            key_s,
            value_s,
            grad_attended.reshape(samples, seq_len, group_width),
            logsums,
            lengths,
        ),
    )
    grad_qkv_rows = jnp.concatenate(
        [
            grad_query.reshape(tokens, group_width),
            grad_key.reshape(tokens, group_width),
            grad_value.reshape(tokens, group_width),
        ],
        axis=1,
    )
    grad_qkv = jnp.einsum(
        "td,tc->dc", normed_one, grad_qkv_rows, preferred_element_type=jnp.float32
    ).reshape(width_model, 3, group_width)
    grad_bias_qv = jnp.stack(
        [
            jnp.sum(grad_query.astype(jnp.float32), axis=(0, 1)),
            jnp.sum(grad_value.astype(jnp.float32), axis=(0, 1)),
        ],
        axis=0,
    )
    normed_one_term = jnp.einsum(
        "tc,dc->td", grad_qkv_rows, qkv_weight, preferred_element_type=jnp.float32
    )
    grad_normed_one = lax.psum(normed_one_term.astype(jnp.bfloat16), "mp").astype(jnp.float32)
    _, first_back = jax.vjp(modulate, inputs, scale_one, shift_one)
    input_norm, grad_scale_one, grad_shift_one = first_back(
        grad_normed_one.reshape(samples, seq_len, width_model)
    )
    grad_latent = (grad_middle + input_norm).reshape(tokens, width_model).astype(jnp.bfloat16)
    grad_modulation = jnp.concatenate(
        [
            grad_shift_one,
            grad_scale_one,
            grad_gate_one,
            grad_shift_two,
            grad_scale_two,
            grad_gate_two,
        ],
        axis=1,
    ).reshape(samples, 6 * width_model)
    part_width = w_ada.shape[1]
    modulation_part = lax.dynamic_slice_in_dim(
        grad_modulation, lax.axis_index("mp") * part_width, part_width, 1
    )
    cond_term = jnp.dot(modulation_part, ada_weight.T, precision=PRECISE)
    grad_silu = lax.psum(cond_term, "mp")
    _, silu_back = jax.vjp(jax.nn.silu, condition.astype(jnp.float32))
    grad_condition = silu_back(grad_silu)[0]
    local_ada = jnp.dot(silu_cond.T, modulation_part, precision=PRECISE)
    local_bias_ada = jnp.sum(modulation_part, axis=0)
    summed = (
        lax.psum(grad_qkv.astype(jnp.bfloat16), "dp").astype(jnp.float32),
        lax.psum(grad_bias_qv.astype(jnp.bfloat16), "dp").astype(jnp.float32),
        lax.psum(grad_out_proj.astype(jnp.bfloat16), "dp").astype(jnp.float32),
        lax.psum(grad_bias_out.astype(jnp.bfloat16), "dp").astype(jnp.float32),
        lax.psum(grad_fc1.astype(jnp.bfloat16), "dp").astype(jnp.float32),
        lax.psum(grad_bias_fc1.astype(jnp.bfloat16), "dp").astype(jnp.float32),
        lax.psum(grad_fc2.astype(jnp.bfloat16), "dp").astype(jnp.float32),
        lax.psum(grad_bias_fc2.astype(jnp.bfloat16), "dp").astype(jnp.float32),
        lax.psum(local_ada.astype(jnp.bfloat16), "dp").astype(jnp.float32),
        lax.psum(local_bias_ada.astype(jnp.bfloat16), "dp").astype(jnp.float32),
    )
    (
        grad_qkv,
        grad_bias_qv,
        grad_out_proj,
        grad_bias_out,
        grad_fc1,
        grad_bias_fc1,
        grad_fc2,
        grad_bias_fc2,
        grad_ada,
        grad_bias_ada,
    ) = summed
    return (
        output,
        grad_latent,
        grad_condition,
        grad_ada,
        grad_bias_ada,
        grad_qkv,
        grad_bias_qv,
        grad_out_proj,
        grad_bias_out,
        grad_fc1,
        grad_bias_fc1,
        grad_fc2,
        grad_bias_fc2,
    )


def solution(mesh):
    return jax.shard_map(
        local,
        mesh=mesh,
        in_specs=(
            P("dp", None),
            P("dp", None),
            P("dp"),
            P(None, "mp"),
            P("mp"),
            P(None, None, "mp"),
            P(None, "mp"),
            P("mp", None),
            P(),
            P(None, "mp"),
            P("mp"),
            P("mp", None),
            P(),
            P("dp", None),
        ),
        out_specs=(
            P("dp", None),
            P("dp", None),
            P("dp", None),
            P(None, "mp"),
            P("mp"),
            P(None, None, "mp"),
            P(None, "mp"),
            P("mp", None),
            P(),
            P(None, "mp"),
            P("mp"),
            P("mp", None),
            P(),
        ),
        check_vma=False,
    )
```

profile of v0, /device:TPU:0, one launch (start us, length us, event | category | flops | bytes accessed | tf_op | source)
XLA Modules:
  0.0 717.0 jit_solution(4267273299513869601)
XLA Ops:
  8.1 2.0 convert_reduce_fusion.2
  10.2 2.4 fusion.24
  15.1 5.4 convolution_reduce_fusion
  20.6 21.0 %all-reduce = f32[6912]{0:T(1024)S(1)} all-reduce(f32[6912]{0:T(1024)S(1)} %add_dynamic-update-slice_fusion), channel_id=2, replica_groups=mesh['dp'=8,'mp'=4] {'mp'}, use_global_device_ids=true, to_apply=%add | all-reduce | flops 6912 | bytes 55296
  41.8 4.9 fusion.60
  47.0 7.5 %fusion.64 = (f32[4,1024]{1,0:T(4,128)S(1)}, f32[4,1024,1024]{1,2,0:T(8,128)}) fusion(bf16[1024,4,72]{0,2,1:T(8,128)(2,1)S(1)} %bitcast.65, bf16[1024,4,72]{0,2,1:T(8,128)(2,1)S(1)} %bitcast.63, pred[1024]{0:T(1024)(128)(4,1)S(1)} %iota_compare_fusion), kind=kOutput, calls=%fused_computation.130 | convolution fusion | flops 616558592 | bytes 17974272 | tf_op jit(solution)/shard_map/while/body/eval_jaxpr/qhd,khd->hqk/dot_general | solution.py:32
  54.5 8.0 %fusion = f32[4,1024]{1,0:T(4,128)S(1)} fusion(f32[4,1024,1024]{1,2,0:T(8,128)} %get-tuple-element.104, f32[4,1024]{1,0:T(4,128)S(1)} %get-tuple-element.103), kind=kLoop, calls=%fused_computation.6 | loop fusion | flops 8384512 | bytes 16809984 | tf_op jit(solution)/shard_map/while/body/eval_jaxpr/reduce_sum | solution.py:49
  62.5 7.5 %fusion.43 = bf16[4,72,1024]{2,1,0:T(8,128)(2,1)S(1)} fusion(bf16[1024,4,72]{0,2,1:T(8,128)(2,1)S(1)} %bitcast.73, f32[4,1024,1024]{1,2,0:T(8,128)} %get-tuple-element.104, f32[4,1024]{1,0:T(4,128)S(1)} %fusion, f32[4,1024]{1,0:T(4,128)S(1)} %get-tuple-element.103), kind=kOutput, calls=%fused_computation.81 | convolution fusion | flops 616857600 | bytes 17989632 | tf_op jit(solution)/shard_map/while/body/eval_jaxpr/hqk,khd->qhd/dot_general | solution.py:51
  70.8 2.9 convolution_convert_fusion.3
  74.1 93.7 %all-reduce.9.cloned.1.call-done = bf16[1024,1152]{1,0:T(8,128)(2,1)} async-done(((bf16[1024,1152]{1,0:T(8,128)(2,1)}), bf16[1024,1152]{1,0:T(8,128)(2,1)}) %all-reduce.9.cloned.1.call-update) | async-done | bytes 2359312 | tf_op jit(solution)/shard_map/psum | solution.py:141
  167.8 3.5 fusion.58
  171.6 1.3 multiply_reduce_fusion.2
  172.9 4.3 convolution_add_fusion
  177.2 5.8 fusion.65
  183.0 1.5 copy-done.50
  184.5 4.8 convolution_convert_fusion.4
  189.3 7.9 %convolution_convert_fusion.5 = bf16[1024,1152]{1,0:T(8,128)(2,1)} fusion(bf16[1152,1152]{1,0:T(8,128)(2,1)S(1)} %copy-done, f32[1024,1152]{1,0:T(8,128)} %copy-done.49), kind=kOutput, calls=%fused_computation.67 | convolution fusion | flops 2729705472 | bytes 9732096 | tf_op jit(solution)/shard_map/dot_general | solution.py:154
  197.3 86.8 %all-reduce.11.cloned.1.call-done = bf16[1024,1152]{1,0:T(8,128)(2,1)} async-done(((bf16[1024,1152]{1,0:T(8,128)(2,1)}), bf16[1024,1152]{1,0:T(8,128)(2,1)}) %all-reduce.11.cloned.1.call-update) | async-done | bytes 2359312 | tf_op jit(solution)/shard_map/psum | solution.py:172
  284.1 5.4 fusion.28
  289.6 2.8 fusion.63
  292.4 1.2 fusion.62
  293.7 0.9 copy-done.8
  294.6 1.4 copy-done.22
  296.0 1.0 convolution_convert_fusion.8
  296.9 8.6 %bitcast_reduce_fusion = (bf16[4,72]{1,0:T(4,128)(2,1)S(1)}, bf16[4,72,1024]{2,1,0:T(8,128)(2,1)S(1)}) fusion(bf16[1024,4,72]{0,2,1:T(8,128)(2,1)S(1)} %bitcast.75, f32[4,1024,1024]{1,2,0:T(8,128)} %get-tuple-element.104, f32[4,1024]{1,0:T(4,128)S(1)} %log_add_fusion), kind=kOutput, calls=%fused_computation.88 | convolution fusion | flops 612957952 | bytes 17973824 | tf_op jit(solution)/shard_map/while/body/eval_jaxpr/hqk,qhd->khd/dot_general | solution.py:67
  305.6 10.9 %multiply_reduce_fusion = (f32[4,1024]{1,0:T(4,128)S(1)}, f32[4,1024,1024]{1,2,0:T(8,128)}) fusion(f32[4,1024,1024]{1,2,0:T(8,128)} %get-tuple-element.104, f32[4,1024]{1,0:T(4,128)S(1)} %log_add_fusion, bf16[1024,4,72]{0,2,1:T(8,128)(2,1)S(1)} %bitcast.76, bf16[1024,4,72]{0,2,1:T(8,128)(2,1)S(1)} %bitcast.74), kind=kOutput, calls=%fused_computation.1 | convolution fusion | flops 616558592 | bytes 34766848 | tf_op jit(solution)/shard_map/while/body/eval_jaxpr/qhd,khd->hqk/dot_general | solution.py:70
  316.5 12.0 %multiply_convert_fusion = bf16[4,1024,1024]{1,2,0:T(8,128)(2,1)S(1)} fusion(f32[4,1024,1024]{1,2,0:T(8,128)} %get-tuple-element.106, f32[4,1024,1024]{1,2,0:T(8,128)} %get-tuple-element.104, f32[4,1024]{1,0:T(4,128)S(1)} %get-tuple-element.105, f32[4,1024]{1,0:T(4,128)S(1)} %log_add_fusion), kind=kLoop, calls=%fused_computation | loop fusion | flops 16777216 | bytes 41975808 | tf_op jit(solution)/shard_map/while/body/eval_jaxpr/convert_element_type | solution.py:74
  328.5 2.7 fusion.39
  331.2 1.7 bitcast_reduce_fusion.1
  333.8 4.1 convolution_convert_fusion.2
  338.6 8.7 %convolution_convert_fusion = bf16[1152,1152]{1,0:T(8,128)(2,1)} fusion(bf16[1024,1152]{1,0:T(8,128)(2,1)} %param.27, f32[1152]{0:T(1024)S(1)} %get-tuple-element.72, f32[1024,1152]{1,0:T(8,128)} %copy-done.49), kind=kOutput, calls=%fused_computation.12 | convolution fusion | flops 2733391872 | bytes 9736704 | tf_op jit(solution)/shard_map/ti,td->id/dot_general | solution.py:163
  347.4 5.5 convolution_convert_fusion.1
  353.1 1.8 convolution_convert_fusion.7
  354.8 4.0 convolution_convert_fusion.6
  358.8 150.6 %all-reduce.15.cloned.1.call-done = (bf16[1024,1152]{1,0:T(8,128)(2,1)}, bf16[1024,1152]{1,0:T(8,128)(2,1)}) async-done(((bf16[1024,1152]{1,0:T(8,128)(2,1)}, bf16[1024,1152]{1,0:T(8,128)(2,1)}), (bf16[1024,1152]{1,0:T(8,128)(2,1)}, bf16[1024,1152]{1,0:T(8,128)(2,1)})) %all-reduce.15.cloned.1.call-update) | async-done | bytes 4718608 | tf_op jit(solution)/shard_map/psum | solution.py:155
  509.5 3.1 fusion.25
  512.6 2.8 fusion.29
  515.4 8.1 %fusion.27 = (f32[1152]{0:T(1024)S(1)}, f32[1152]{0:T(1024)S(1)}, bf16[1024,1152]{1,0:T(8,128)(2,1)}, bf16[1024,1152]{1,0:T(8,128)(2,1)}) fusion(bf16[1024,1152]{1,0:T(8,128)(2,1)S(1)} %copy-done.13, bf16[1024,1152]{1,0:T(8,128)(2,1)S(1)} %copy-done.24, f32[1152]{0:T(1024)S(1)} %convert_element_type.213, f32[1152]{0:T(1024)S(1)} %convert_element_type.207, ...), kind=kLoop, calls=%fused_computation.51 | loop fusion | flops 31848192 | bytes 21286400 | tf_op jit(solution)/shard_map/reduce_sum | solution.py:161
  523.7 2.5 multiply_convert_fusion.1
  526.4 25.3 %all-reduce.1 = (bf16[1728]{0:T(1024)(128)(2,1)S(1)}, bf16[2,288]{1,0:T(2,128)(2,1)S(1)}, bf16[1152]{0:T(1024)(128)(2,1)S(1)}, bf16[1152]{0:T(1024)(128)(2,1)S(1)}, bf16[1152]{0:T(1024)(128)(2,1)S(1)}) all-reduce(bf16[1728]{0:T(1024)(128)(2,1)S(1)} %convert_element_type.235, ...), channel_id=1, replica_groups=mesh['dp'=8,'mp'=4] {'dp'}, use_global_device_ids=true, to_apply=%region_23.24 | all-reduce | flops 5760 | bytes 23040 | tf_op jit(solution)/shard_map/psum | solution.py:254
  554.7 4.2 fusion.46
  558.9 9.9 %psum.109 = f32[1,1152]{1,0:T(1,128)S(1)} all-reduce(f32[1,1152]{1,0:T(1,128)S(1)} %fusion.46), channel_id=1, replica_groups=mesh['dp'=8,'mp'=4] {'mp'}, use_global_device_ids=true, to_apply=%region_21.22 | all-reduce | flops 1152 | bytes 9216 | tf_op jit(solution)/shard_map/psum | solution.py:239
  569.4 124.0 %all-reduce.13.cloned.1.call-done = (bf16[1152,1728]{0,1:T(8,128)(2,1)}, bf16[1152,3,288]{0,2,1:T(8,128)(2,1)}, bf16[288,1152]{1,0:T(8,128)(2,1)}, bf16[1152,1152]{1,0:T(8,128)(2,1)}, bf16[1152,1152]{1,0:T(8,128)(2,1)}) async-done(((bf16[1152,1728]{0,1:T(8,128)(2,1)}, bf16[1152,3,288]{0,2,1:T(8,128)(2,1)}, bf16[288,1152]{1,0:T(8,128)(2,1)}, bf16[1152,1152]{1,0:T(8,128)(2,1)}, bf16[1152,1152]{1,0:T(8,128)(2,1)}), ...) | async-done | bytes 11943952 | tf_op jit(solution)/shard_map/psum | solution.py:253
  693.4 2.2 convert_element_type.243
  695.7 6.0 convert_element_type.234
  701.7 2.2 convert_element_type.238
  704.8 2.7 convert_element_type.246
  707.5 2.7 convert_element_type.249
  (151 shorter events, 10.5 us)
Async XLA Ops:
  7.2 170.0 %copy-start = (bf16[1152,1152]{1,0:T(8,128)(2,1)S(1)}, bf16[1152,1152]{1,0:T(8,128)(2,1)}, u32[]{:S(2)}) copy-start(bf16[1152,1152]{1,0:T(8,128)(2,1)} %param.25) | copy-start | bytes 7962628
  7.2 6.7 copy-start.48
  7.2 6.0 copy-start.37
  7.2 6.0 copy-start.30
  7.2 13.3 %copy-start.41 = (bf16[1728]{0:T(1024)(128)(2,1)S(1)}, bf16[1728]{0:T(1024)(128)(2,1)}, u32[]{:S(2)}) copy-start(bf16[1728]{0:T(1024)(128)(2,1)} %param.18) | copy-start | bytes 10372
  7.2 160.6 %all-reduce.9.cloned.1.call-start = ((), (), s32[]{:S(2)}) async-start(), calls=%async_computation | async-start | bytes 4718592 | tf_op jit(solution)/shard_map/psum | solution.py:141
  13.9 6.6 copy-start.32
  47.0 7.5 %copy-start.14 = (bf16[1024,288]{0,1:T(8,128)(2,1)}, bf16[1024,288]{0,1:T(8,128)(2,1)S(1)}, u32[]{:S(2)}) copy-start(bf16[1024,288]{0,1:T(8,128)(2,1)S(1)} %get-tuple-element.100) | copy-start | bytes 1769476
  47.0 15.5 %copy-start.27 = (bf16[1024,288]{0,1:T(8,128)(2,1)}, bf16[1024,288]{0,1:T(8,128)(2,1)S(1)}, u32[]{:S(2)}) copy-start(bf16[1024,288]{0,1:T(8,128)(2,1)S(1)} %get-tuple-element.101) | copy-start | bytes 1769476
  62.5 8.3 %copy-start.44 = (bf16[288,1152]{1,0:T(8,128)(2,1)S(1)}, bf16[288,1152]{1,0:T(8,128)(2,1)}, u32[]{:S(2)}) copy-start(bf16[288,1152]{1,0:T(8,128)(2,1)} %param.21) | copy-start | bytes 1990660
  70.0 4.0 copy-start.38
  70.0 4.0 copy-start.39
  73.8 210.3 %all-reduce.11.cloned.1.call-start = ((), (), s32[]{:S(2)}) async-start(), calls=%async_computation.1 | async-start | bytes 4718592 | tf_op jit(solution)/shard_map/psum | solution.py:172
  167.8 3.5 copy-start.2
  167.8 3.8 copy-start.4
  167.8 5.1 copy-start.42
  172.9 4.3 copy-start.11
  177.2 5.8 copy-start.49
  189.3 320.2 %all-reduce.15.cloned.1.call-start = ((), (), s32[]{:S(2)}) async-start(), calls=%async_computation.3 | async-start | bytes 9437184 | tf_op jit(solution)/shard_map/psum | solution.py:155
  197.3 92.3 %copy-start.3 = (bf16[1024,1152]{1,0:T(8,128)(2,1)S(1)}, bf16[1024,1152]{1,0:T(8,128)(2,1)}, u32[]{:S(2)}) copy-start(bf16[1024,1152]{1,0:T(8,128)(2,1)} %param.14) | copy-start | bytes 7077892
  284.1 5.5 copy-start.5
  284.1 5.5 copy-start.10
  289.6 2.8 copy-start.12
  292.4 3.6 copy-start.45
  296.9 8.6 %copy-start.28 = (bf16[1024,288]{0,1:T(8,128)(2,1)S(1)}, bf16[1024,288]{0,1:T(8,128)(2,1)}, u32[]{:S(2)}) copy-start(bf16[1024,288]{0,1:T(8,128)(2,1)} %copy-done.27) | copy-start | bytes 1769476
  305.6 27.4 %copy-start.25 = (bf16[4,72,1024]{2,1,0:T(8,128)(2,1)}, bf16[4,72,1024]{2,1,0:T(8,128)(2,1)S(1)}, u32[]{:S(2)}) copy-start(bf16[4,72,1024]{2,1,0:T(8,128)(2,1)S(1)} %get-tuple-element.108) | copy-start | bytes 1769476
  316.5 12.0 %copy-start.15 = (bf16[1024,288]{0,1:T(8,128)(2,1)S(1)}, bf16[1024,288]{0,1:T(8,128)(2,1)}, u32[]{:S(2)}) copy-start(bf16[1024,288]{0,1:T(8,128)(2,1)} %copy-done.14) | copy-start | bytes 1769476
  331.2 2.6 copy-start.43
  338.0 355.5 %all-reduce.13.cloned.1.call-start = ((), (), s32[]{:S(2)}) async-start(), calls=%async_computation.2 | async-start | bytes 23887872 | tf_op jit(solution)/shard_map/psum | solution.py:253
  338.6 8.7 %copy-start.6 = (bf16[1024,1152]{1,0:T(8,128)(2,1)S(1)}, bf16[1024,1152]{1,0:T(8,128)(2,1)}, u32[]{:S(2)}) copy-start(bf16[1024,1152]{1,0:T(8,128)(2,1)} %all-reduce.9.cloned.1.call-done) | copy-start | bytes 7077892
  338.6 8.7 %copy-start.51 = (bf16[1024,1152]{1,0:T(8,128)(2,1)S(1)}, bf16[1024,1152]{1,0:T(8,128)(2,1)}, u32[]{:S(2)}) copy-start(bf16[1024,1152]{1,0:T(8,128)(2,1)} %copy-done.50) | copy-start | bytes 7077892
  347.4 5.5 copy-start.19
  347.4 5.5 copy-start.21
  347.4 5.5 copy-start.26
  347.4 5.7 copy-start.23
  347.4 5.7 copy-start.47
  358.8 153.7 %copy-start.35 = (f32[1024]{0:T(1024)S(1)}, f32[1024]{0:T(1024)}, u32[]{:S(2)}) copy-start(f32[1024]{0:T(1024)} %copy-done.34) | copy-start | bytes 12292
  509.5 3.1 copy-start.9
  509.5 5.9 copy-start.7
  509.5 5.9 copy-start.13
  509.5 5.9 copy-start.24
  515.4 8.3 %copy-start.36 = (f32[1152]{0:T(1024)S(1)}, f32[1152]{0:T(1024)}, u32[]{:S(2)}) copy-start(f32[1152]{0:T(1024)} %get-tuple-element.94) | copy-start | bytes 13828
  526.2 42.6 %copy-start.31 = (bf16[1,1152]{1,0:T(2,128)(2,1)S(1)}, bf16[1,1152]{1,0:T(2,128)(2,1)}, u32[]{:S(2)}) copy-start(bf16[1,1152]{1,0:T(2,128)(2,1)} %param.15) | copy-start | bytes 6916
  526.2 42.6 %copy-start.33 = (f32[1,1152]{1,0:T(1,128)S(1)}, f32[1,1152]{1,0:T(1,128)}, u32[]{:S(2)}) copy-start(f32[1,1152]{1,0:T(1,128)} %copy-done.32) | copy-start | bytes 13828
  695.7 6.0 copy-start.29
  701.7 3.1 copy-start.17
  703.9 3.6 copy-start.16
  704.8 5.5 copy-start.1
  (8 other events, 9.8 us)
Sparse Core Ops, SparseCore 0:
  73.9 93.8 all-reduce.8
  189.4 94.6 all-reduce.10
  338.1 171.3 all-reduce.14
  526.3 167.0 all-reduce.12
where the time goes:
time: 720 us; the launch traced here: 717 us
  waiting for transfers between devices  455 us (63%)
  matrix products  104 us (14%)
  other arithmetic  75.9 us (11%)
  blocking collectives  56.3 us (8%)
  between operations  16.2 us (2%)
  local copies, waits for them, and re-layouts  8.92 us (1%)
    psum x1, waiting for transfers between devices, local(): lax.psum(mlp_term.astype(jnp.bfloat16), 'mp').astype(jnp.float32)  151 us
    psum x1, waiting for transfers between devices, local(): lax.psum(local_ada.astype(jnp.bfloat16), 'dp').astype(jnp.float32)  124 us
    psum x1, waiting for transfers between devices, local(): lax.psum(attn_term.astype(jnp.bfloat16), 'mp').astype(jnp.float32)  93.7 us
    psum x1, waiting for transfers between devices, local(): lax.psum(normed_two_term.astype(jnp.bfloat16), 'mp').astype(jnp.float32)  86.8 us
    psum x1, blocking collectives, local(): lax.psum(local_bias_ada.astype(jnp.bfloat16), 'dp').astype(jnp.float32)  25.3 us
    unnamed x1, blocking collectives  21 us
  transfers between devices with their start and end apart: 4, of which 4 were waited for; matrix products, arithmetic and copies ran while one was open for 5% of the time, Pallas kernels for 0%

commit v1 on v0

v1 whole, which is shorter than its diff:
```python
import math

import jax
import jax.numpy as jnp
from jax import lax
from jax.experimental import pallas as pl
from jax.experimental.pallas import tpu as pltpu
from jax.sharding import PartitionSpec as P

HD = 72
HP = 128
EPSILON = 1e-06
F32 = jnp.float32
BF16 = jnp.bfloat16
PRECISE = lax.Precision.HIGHEST
LOG2E = math.log2(math.e)
SCORE = LOG2E / math.sqrt(HD)
SCALING = 1.0 / math.sqrt(HD)
MIB = 1 << 20
NT = (((1,), (1,)), ((), ()))
TN = (((0,), (0,)), ((), ()))
IN_HOP = ((0, 1), (3, 2))
MID_HOP = ((1, 2), (2, 1))
OUT_HOP = ((1, 0), (2, 3))
SHIFT_A, SCALE_A, GATE_A, SHIFT_M, SCALE_M, GATE_M = range(6)


def dot(a, b):
    return jnp.dot(a, b, preferred_element_type=F32)


def dot_nt(a, b):
    return lax.dot_general(a, b, NT, preferred_element_type=F32)


def dot_tn(a, b):
    return lax.dot_general(a, b, TN, preferred_element_type=F32)


def params(mib):
    return pltpu.CompilerParams(vmem_limit_bytes=mib * MIB)


def cost(flops, size):
    return pl.CostEstimate(flops=int(flops), bytes_accessed=int(size), transcendentals=0)


def normalize(values):
    row_mean = jnp.mean(values, axis=-1, keepdims=True)
    centred = values - row_mean
    inverse = lax.rsqrt(jnp.mean(centred * centred, axis=-1, keepdims=True) + EPSILON)
    return centred * inverse, inverse


def normalize_back(normal, inverse, grad):
    mean_grad = jnp.mean(grad, axis=-1, keepdims=True)
    mean_both = jnp.mean(grad * normal, axis=-1, keepdims=True)
    return inverse * (grad - mean_grad - normal * mean_both)


def total(values):
    return jnp.sum(values, axis=0, keepdims=True)


def full(shape, dtype):
    return jax.ShapeDtypeStruct(shape, dtype)


def call(kernel, index, inputs, outputs, scalars=(), name=None, mib=32, flops=0, size=0):
    operands, in_specs, out_specs, shapes, aliases = [], [], [], [], {}

    def spec(shape, rows):
        if rows is None:
            return pl.BlockSpec(shape, lambda i, *_: (0,) * len(shape))
        if rows == "lanes":
            return pl.BlockSpec((shape[0], BLOCK_LANES), lambda i, *_: (0, index))
        return pl.BlockSpec((rows, *shape[1:]), lambda i, *_: (index, 0))

    for value, rows in inputs:
        operands.append(value)
        in_specs.append(spec(value.shape, rows))
    count = len(operands)
    for place, (shape, rows, buffer) in enumerate(outputs):
        shapes.append(shape)
        out_specs.append(spec(shape.shape, rows))
        if buffer is not None:
            aliases[len(scalars) + len(operands)] = place
            operands.append(buffer)
            in_specs.append(pl.BlockSpec(memory_space=pl.ANY))
    held = len(operands) - count

    def body(*refs):
        refs = list(refs)
        del refs[len(scalars) + count : len(scalars) + count + held]
        kernel(*refs)

    return pl.pallas_call(
        body,
        out_shape=shapes,
        grid_spec=pltpu.PrefetchScalarGridSpec(
            num_scalar_prefetch=len(scalars), grid=(1,), in_specs=in_specs, out_specs=out_specs
        ),
        input_output_aliases=aliases,
        compiler_params=params(mib),
        cost_estimate=cost(flops, size),
        name=name,
    )(*scalars, *operands)


BLOCK_LANES = 256


def thirds(values):
    high = values.astype(BF16).astype(F32)
    rest = values - high
    middle = rest.astype(BF16).astype(F32)
    return high, middle, rest - middle


def modulate_kernel(cond_ref, w_ref, b_ref, out_ref):
    step = pl.program_id(0)
    cond = cond_ref[...].astype(F32)
    rows = jnp.concatenate([*thirds(cond / (1.0 + jnp.exp(-cond))), jnp.zeros((5, cond.shape[1]), F32)])
    part = total(dot(rows.astype(BF16), w_ref[...]))

    @pl.when(step == 0)
    def _():
        out_ref[...] = b_ref[...].astype(F32) + part

    @pl.when(step > 0)
    def _():
        out_ref[...] += part


def modulate(condition, weight, bias):
    model, wide = weight.shape
    step = 384
    return pl.pallas_call(
        modulate_kernel,
        out_shape=full((1, wide), F32),
        grid=(model // step,),
        in_specs=[
            pl.BlockSpec((1, step), lambda i: (0, i)),
            pl.BlockSpec((step, wide), lambda i: (i, 0)),
            pl.BlockSpec((1, wide), lambda i: (0, 0)),
        ],
        out_specs=pl.BlockSpec((1, wide), lambda i: (0, 0)),
        compiler_params=params(16),
        cost_estimate=cost(16 * model * wide, 2 * model * wide),
        name="modulate",
    )(condition, weight, bias.reshape(1, wide))


def condition_kernel(grad_ref, w_ref, out_ref):
    grad = grad_ref[...]
    rows = jnp.concatenate([*thirds(grad), jnp.zeros((5, grad.shape[1]), F32)])
    out_ref[...] = total(dot_nt(rows.astype(BF16), w_ref[...]))


def condition_term(grad, weight):
    model, wide = weight.shape
    step = 384
    return pl.pallas_call(
        condition_kernel,
        out_shape=full((1, model), F32),
        grid=(model // step,),
        in_specs=[
            pl.BlockSpec((1, wide), lambda i: (0, 0)),
            pl.BlockSpec((step, wide), lambda i: (i, 0)),
        ],
        out_specs=pl.BlockSpec((1, step), lambda i: (0, i)),
        compiler_params=params(16),
        cost_estimate=cost(16 * model * wide, 2 * model * wide),
        name="condition_term",
    )(grad, weight)


def outer_kernel(a_ref, b_ref, out_ref):
    a, b = thirds(a_ref[...]), thirds(b_ref[...])
    left = jnp.concatenate([a[0], a[0], a[1], a[0], a[1], a[2]]).astype(BF16)
    right = jnp.concatenate([b[0], b[1], b[0], b[2], b[1], b[0]]).astype(BF16)
    out_ref[...] = dot_tn(left, right)


def outer(a, b):
    samples, model = a.shape
    wide = b.shape[1]
    step = 384
    return pl.pallas_call(
        outer_kernel,
        out_shape=full((model, wide), F32),
        grid=(model // step,),
        in_specs=[
            pl.BlockSpec((samples, step), lambda i: (0, i)),
            pl.BlockSpec((samples, wide), lambda i: (0, 0)),
        ],
        out_specs=pl.BlockSpec((step, wide), lambda i: (i, 0)),
        compiler_params=params(24),
        cost_estimate=cost(12 * samples * model * wide, 4 * model * wide),
        name="outer",
    )(a, b)


def spread(ref, values, heads, extra=None):
    ref[...] = jnp.zeros_like(ref)
    for head in range(heads):
        ref[:, head * HP : head * HP + HD] = values[:, head * HD : (head + 1) * HD].astype(BF16)
        if extra is not None:
            ref[:, head * HP + HD : head * HP + HD + 1] = extra


def project_kernel(len_ref, lat_ref, mod_ref, w_ref, b_ref, n_ref, q_ref, k_ref, v_ref):
    rows, width = q_ref.shape
    heads = width // HP
    group = heads * HD
    first = pl.program_id(0) * rows
    normal, _ = normalize(lat_ref[...].astype(F32))
    scale = 1.0 + mod_ref[SCALE_A : SCALE_A + 1, :]
    normed = (normal * scale + mod_ref[SHIFT_A : SHIFT_A + 1, :]).astype(BF16)
    n_ref[...] = normed
    found = dot(normed, w_ref[...]) + b_ref[...]
    ones = jnp.ones((rows, 1), BF16)
    row = lax.broadcasted_iota(jnp.int32, (rows, 1), 0) + first
    hidden = jnp.where(row >= len_ref[0], -1e30, 0.0).astype(BF16)
    spread(q_ref, found[:, :group], heads, ones)
    spread(k_ref, found[:, group : 2 * group], heads, hidden)
    spread(v_ref, found[:, 2 * group :], heads, ones)


def project(lengths, latent, mod, weight, bias, block):
    tokens, model = latent.shape
    width = weight.shape[1] // 3 // HD * HP
    rows = lambda i, *_: (i, 0)
    whole = lambda i, *_: (0, 0)
    return pl.pallas_call(
        project_kernel,
        out_shape=[full((tokens, model), BF16)] + [full((tokens, width), BF16)] * 3,
        grid_spec=pltpu.PrefetchScalarGridSpec(
            num_scalar_prefetch=1,
            grid=(tokens // block,),
            in_specs=[
                pl.BlockSpec((block, model), rows),
                pl.BlockSpec(mod.shape, whole),
                pl.BlockSpec(weight.shape, whole),
                pl.BlockSpec(bias.shape, whole),
            ],
            out_specs=[pl.BlockSpec((block, model), rows)]
            + [pl.BlockSpec((block, width), rows)] * 3,
        ),
        compiler_params=params(32),
        cost_estimate=cost(6 * tokens * model * width, tokens * model * 8),
        name="project",
    )(lengths, latent, mod, weight, bias)


def attend_kernel(q_ref, k_ref, v_ref, wo_ref, term_ref, att_ref, mix_ref, lse_ref):
    rows, width = q_ref.shape
    lane = lax.broadcasted_iota(jnp.int32, (rows, HP), 1)
    stats = jnp.zeros((rows, HP), F32)
    for head in range(width // HP):
        at = slice(head * HP, (head + 1) * HP)
        scores = dot_nt(q_ref[:, at], k_ref[:, at])
        top = jnp.max(scores, axis=-1, keepdims=True)
        weights = jnp.exp2((scores - top) * SCORE).astype(BF16)
        mixed = dot(weights, v_ref[:, at])
        row_total = mixed[:, HD : HD + 1]
        mixed = mixed / row_total
        mix_ref[:, at] = mixed
        att_ref[:, head * HD : (head + 1) * HD] = mixed[:, :HD].astype(BF16)
        stats = jnp.where(lane == head, top * SCORE + jnp.log2(row_total), stats)
    lse_ref[...] = stats.T[: lse_ref.shape[0], :]
    term_ref[...] = dot(att_ref[...], wo_ref[...]).astype(BF16)


def attend(query, key, value, w_out, held, index, block):
    tokens, width = query.shape
    group, model = w_out.shape
    return call(
        attend_kernel, index,
        [(query, block), (key, None), (value, None), (w_out, None)],
        [
            (full((block, model), BF16), None, None),
            (full((tokens, group), BF16), block, held[0]),
            (full((tokens, width), F32), block, held[1]),
            (full((8, tokens), F32), "lanes", held[2]),
        ],
        name="attend", flops=4 * block * tokens * width, size=6 * tokens * width,
    )


def feed_kernel(
    end_ref, near_ref, far_ref, lat_ref, cot_ref, mod_ref, bo_ref, w1_ref, b1_ref, w2_ref,
    term_ref, sum_ref, tot_ref, n_ref, act_ref, gh_ref, gm_ref,
):
    summed = jnp.where(end_ref[0] == 1, far_ref[...].astype(F32), near_ref[...].astype(F32))
    tot_ref[...] = summed.astype(BF16)
    branch = summed + bo_ref[...]
    middle = lat_ref[...].astype(F32) + mod_ref[GATE_A : GATE_A + 1, :] * branch
    normal, _ = normalize(middle)
    scale = 1.0 + mod_ref[SCALE_M : SCALE_M + 1, :]
    normed = (normal * scale + mod_ref[SHIFT_M : SHIFT_M + 1, :]).astype(BF16)
    n_ref[...] = normed
    grad_mlp = (mod_ref[GATE_M : GATE_M + 1, :] * cot_ref[...].astype(F32)).astype(BF16)
    gm_ref[...] = grad_mlp
    hidden = dot(normed, w1_ref[...]) + b1_ref[...]
    grad_act = dot_nt(grad_mlp, w2_ref[...])
    root = math.sqrt(2.0 / math.pi)
    square = hidden * hidden
    bend = jnp.tanh(root * hidden * (1.0 + 0.044715 * square))
    half = 0.5 * (1.0 + bend)
    act_ref[...] = (hidden * half).astype(BF16)
    slope = half + 0.5 * hidden * (1.0 - bend * bend) * (root * (1.0 + 3 * 0.044715 * square))
    grad_hidden = (slope * grad_act).astype(BF16)
    gh_ref[...] = grad_hidden
    sum_ref[0:1, :] = total(grad_hidden.astype(F32))
    term_ref[...] = dot_nt(grad_hidden, w1_ref[...]).astype(BF16)


def feed(end, near, far, latent, cotangent, mod, b_out, w_fc1, b_fc1, w_fc2, held, index, block):
    model, hidden = w_fc1.shape
    tokens = latent.shape[0]
    return call(
        feed_kernel, index,
        [
            (near, None), (far, None), (latent, block), (cotangent, block), (mod, None),
            (b_out, None), (w_fc1, None), (b_fc1, None), (w_fc2, None),
        ],
        [
            (full((block, model), BF16), None, None),
            (full((8, hidden), F32), None, None),
            (full((tokens, model), BF16), block, held[0]),
            (full((tokens, model), BF16), block, held[1]),
            (full((tokens, hidden), BF16), block, held[2]),
            (full((tokens, hidden), BF16), block, held[3]),
            (full((tokens, model), BF16), block, held[4]),
        ],
        scalars=(end,), name="feed", mib=40,
        flops=6 * block * model * hidden, size=4 * model * hidden + 12 * block * model,
    )


def middle_kernel(
    end_ref, near_ref, far_ref, tot_ref, lat_ref, cot_ref, mod_ref, bo_ref, wo_ref,
    sum_ref, ga_ref, gmid_ref, datt_ref,
):
    grad = jnp.where(end_ref[0] == 1, far_ref[...].astype(F32), near_ref[...].astype(F32))
    branch = tot_ref[...].astype(F32) + bo_ref[...]
    gate = mod_ref[GATE_A : GATE_A + 1, :]
    normal, inverse = normalize(lat_ref[...].astype(F32) + gate * branch)
    sum_ref[0:1, :] = total(grad)
    sum_ref[1:2, :] = total(grad * normal)
    scale = 1.0 + mod_ref[SCALE_M : SCALE_M + 1, :]
    grad_middle = cot_ref[...].astype(F32) + normalize_back(normal, inverse, grad * scale)
    gmid_ref[...] = grad_middle
    sum_ref[2:3, :] = total(grad_middle * branch)
    grad_attn = (gate * grad_middle).astype(BF16)
    ga_ref[...] = grad_attn
    sum_ref[3:4, :] = total(grad_attn.astype(F32))
    spread(datt_ref, dot_nt(grad_attn, wo_ref[...]), datt_ref.shape[1] // HP)


def middle_back(end, near, far, tot, latent, cotangent, mod, b_out, w_out, held, index, block):
    group, model = w_out.shape
    width = group // HD * HP
    tokens = latent.shape[0]
    return call(
        middle_kernel, index,
        [
            (near, None), (far, None), (tot, block), (latent, block), (cotangent, block),
            (mod, None), (b_out, None), (w_out, None),
        ],
        [
            (full((8, model), F32), None, None),
            (full((tokens, model), BF16), block, held[0]),
            (full((tokens, model), F32), block, held[1]),
            (full((tokens, width), BF16), block, held[2]),
        ],
        scalars=(end,), name="middle", flops=2 * block * model * width, size=16 * block * model,
    )


def attend_back_kernel(q_ref, k_ref, v_ref, do_ref, mix_ref, lse_ref, dq_ref, dk_ref, dv_ref, sk, sv, *, first):
    head = pl.program_id(0) + first
    tokens = q_ref.shape[0]
    block = 256
    key, value = k_ref[...], v_ref[...]

    def step(i, carry):
        at = pl.ds(pl.multiple_of(i * block, block), block)
        query, grad = q_ref[at, :], do_ref[at, :]
        both = grad.astype(F32) * mix_ref[at, :]
        inner = jnp.sum(both.T, axis=0, keepdims=True)
        prob = jnp.exp2(dot_nt(key, query) * SCORE - lse_ref[pl.ds(head, 1), at])
        grad_score = (prob * (dot_nt(value, grad) - inner)).astype(BF16)
        sv[...] += dot(prob.astype(BF16), grad)
        sk[...] += dot(grad_score, query)
        dq_ref[at, :] = (dot_tn(grad_score, key) * SCALING).astype(BF16)
        return carry

    sk[...] = jnp.zeros_like(sk)
    sv[...] = jnp.zeros_like(sv)
    lax.fori_loop(0, tokens // block, step, 0)
    dk_ref[...] = (sk[...] * SCALING).astype(BF16)
    dv_ref[...] = sv[...].astype(BF16)


def attend_back(query, key, value, grad, mixed, lse, first, heads):
    tokens, width = query.shape
    mine = pl.BlockSpec((tokens, HP), lambda h: (0, h + first))
    made = pl.BlockSpec((tokens, HP), lambda h: (0, h))
    width = heads * HP

    def attend_back_body(*refs):
        attend_back_kernel(*refs, first=first)

    return pl.pallas_call(
        attend_back_body,
        out_shape=[full((tokens, width), BF16)] * 3,
        grid=(heads,),
        in_specs=[mine] * 5 + [pl.BlockSpec(lse.shape, lambda h: (0, 0))],
        out_specs=[made] * 3,
        scratch_shapes=[pltpu.VMEM((tokens, HP), F32)] * 2,
        compiler_params=params(32),
        cost_estimate=cost(10 * tokens * tokens * width, 18 * tokens * width),
        name="attend_back",
    )(query, key, value, grad, mixed, lse)


def first_kernel(*refs):
    *parts, w_ref, lat_ref, term_ref, sum_ref, pack_ref = refs
    group = pack_ref.shape[1] // 3
    halves = len(parts) // 3
    for which in range(3):
        at = which * group
        for half in range(halves):
            ref = parts[half * 3 + which]
            for head in range(ref.shape[1] // HP):
                pack_ref[:, at : at + HD] = ref[:, head * HP : head * HP + HD]
                at += HD
    term = dot_nt(pack_ref[...], w_ref[...]).astype(BF16)
    term_ref[...] = term
    normal, _ = normalize(lat_ref[...].astype(F32))
    term = term.astype(F32)
    sum_ref[0:1, :] = total(term)
    sum_ref[1:2, :] = total(term * normal)


def first_term(parts, weight, latent, held, index, block):
    model, wide = weight.shape
    tokens = latent.shape[0]
    return call(
        first_kernel, index,
        [(v, block) for v in parts] + [(weight, None), (latent, block)],
        [
            (full((block, model), BF16), None, None),
            (full((8, model), F32), None, None),
            (full((tokens, wide), BF16), block, held),
        ],
        name="first_term", flops=2 * block * model * wide, size=2 * model * wide,
    )


def final_kernel(end_ref, near_ref, far_ref, lat_ref, gmid_ref, mod_ref, out_ref):
    grad = jnp.where(end_ref[0] == 1, far_ref[...].astype(F32), near_ref[...].astype(F32))
    normal, inverse = normalize(lat_ref[...].astype(F32))
    scale = 1.0 + mod_ref[SCALE_A : SCALE_A + 1, :]
    out_ref[...] = (gmid_ref[...] + normalize_back(normal, inverse, grad * scale)).astype(BF16)


def final(end, near, far, latent, grad_middle, mod, held, index, block):
    return call(
        final_kernel, index,
        [(near, None), (far, None), (latent, block), (grad_middle, block), (mod, None)],
        [(full(latent.shape, BF16), block, held)],
        scalars=(end,), name="final", mib=24, size=12 * block * latent.shape[1],
    )


def output_kernel(end_ref, near_ref, far_ref, tot_ref, lat_ref, cot_ref, mod_ref, bo_ref, b2_ref, sum_ref, out_ref):
    branch = jnp.where(end_ref[0] == 1, far_ref[...].astype(F32), near_ref[...].astype(F32))
    branch += b2_ref[...]
    attn = tot_ref[...].astype(F32) + bo_ref[...]
    middle = lat_ref[...].astype(F32) + mod_ref[GATE_A : GATE_A + 1, :] * attn
    out_ref[...] = (middle + mod_ref[GATE_M : GATE_M + 1, :] * branch).astype(BF16)
    sum_ref[0:1, :] = total(cot_ref[...].astype(F32) * branch)


def output_rows(end, near, far, tot, latent, cotangent, mod, b_out, b_fc2, held, index, block):
    model = latent.shape[1]
    return call(
        output_kernel, index,
        [
            (near, None), (far, None), (tot, block), (latent, block), (cotangent, block),
            (mod, None), (b_out, None), (b_fc2, None),
        ],
        [(full((8, model), F32), None, None), (full(latent.shape, BF16), block, held)],
        scalars=(end,), name="output", mib=24, size=12 * block * model,
    )


def add_kernel(a_ref, b_ref, o_ref):
    o_ref[...] = (a_ref[...].astype(F32) + b_ref[...].astype(F32)).astype(BF16)


def add(a, b):
    return pl.pallas_call(
        add_kernel,
        out_shape=jax.ShapeDtypeStruct(a.shape, BF16),
        compiler_params=params(8),
        cost_estimate=cost(a.size, 6 * a.size),
        name="add",
    )(a, b)


class Order:
    def __init__(self):
        self.last = None

    def __call__(self, step, *values):
        if self.last is not None:
            *values, _ = lax.optimization_barrier((*values, self.last))
        result = step(*values)
        self.last = result[0] if isinstance(result, (tuple, list)) else result
        return result


def build(groups, replicas):
    line = groups == 4

    def hop(value, pairs):
        return lax.ppermute(value, "mp", pairs)

    def gather_groups(value):
        if not line:
            return lax.all_gather(value, "mp", axis=0)
        rank = lax.axis_index("mp")
        turned = [value] + [hop(value, [(j, (j - d) % 4) for j in range(4)]) for d in (1, 2, 3)]
        turned = jnp.stack(turned + turned)
        return lax.dynamic_slice_in_dim(turned, (4 - rank) % 4, 4, 0)

    def local(
        latent, condition, lengths, w_ada, b_ada, w_qkv, b_qv, w_out, b_out,
        w_fc1, b_fc1, w_fc2, b_fc2, cotangent,
    ):
        tokens, model = latent.shape
        group = w_qkv.shape[2]
        heads = group // HD
        chunks = tokens // BLOCK_LANES
        block = BLOCK_LANES
        rank = lax.axis_index("mp")
        order = Order()
        part_width = w_ada.shape[1]

        mod_part = modulate(condition, w_ada, b_ada)
        modulation = gather_groups(mod_part).reshape(6, model)
        mod = jnp.pad(modulation, ((0, 2), (0, 0)))
        end = ((rank == 0) | (rank == groups - 1)).astype(jnp.int32).reshape(1)
        if not line:
            end = jnp.zeros((1,), jnp.int32)

        qkv_weight = w_qkv.reshape(model, 3 * group)
        qv_bias = b_qv.astype(F32)
        qkv_bias = jnp.concatenate([qv_bias[0], jnp.zeros((group,), F32), qv_bias[1]]).reshape(1, -1)
        out_bias = b_out.astype(F32).reshape(1, model)
        fc1_bias = b_fc1.astype(F32).reshape(1, -1)
        fc2_bias = b_fc2.astype(F32).reshape(1, model)

        normed_one, query, key, value = project(lengths, latent, mod, qkv_weight, qkv_bias, block)
        order.last = normed_one

        terms, first, mid, near, far = {}, {}, {}, {}, {}

        def send(job, term):
            terms[job] = term
            if line:
                first[job] = hop(term, IN_HOP)
            else:
                near[job] = far[job] = lax.psum(term, "mp")

        def relay(job):
            if line:
                mid[job] = order(add, terms[job], first[job])
                first[job] = hop(mid[job], MID_HOP)

        def spread_out(job):
            if line:
                near[job] = order(add, mid[job], first[job])
                far[job] = hop(near[job], OUT_HOP)

        state = {
            "att": (None,) * 3, "feed": (None,) * 5, "mid": (None,) * 3, "first": None,
            "final": None, "out": None, "hidden": [], "middle": [], "ends": [], "gate": [],
        }

        def do_attend(k):
            term, *state["att"] = order(
                lambda q, *held: attend(q, key, value, w_out, held or (None,) * 3, k, block),
                query, *[v for v in state["att"] if v is not None],
            )
            send(("a", k), term)

        def do_feed(k):
            term, sums, *state["feed"] = order(
                lambda a, b, *held: feed(
                    end, a, b, latent, cotangent, mod, out_bias, w_fc1, fc1_bias, w_fc2,
                    held or (None,) * 5, k, block,
                ),
                near["a", k], far["a", k], *[v for v in state["feed"] if v is not None],
            )
            state["hidden"].append(sums[0:1])
            send(("g", k), term)

        def do_middle(k):
            sums, *state["mid"] = order(
                lambda a, b, *held: middle_back(
                    end, a, b, state["feed"][0], latent, cotangent, mod, out_bias, w_out,
                    held or (None,) * 3, k, block,
                ),
                near["g", k], far["g", k], *[v for v in state["mid"] if v is not None],
            )
            state["middle"].append(sums)

        def do_back(start, count):
            return order(
                lambda g: attend_back(query, key, value, g, *state["att"][1:], start, count),
                state["mid"][2],
            )

        def do_first(k, parts):
            term, sums, state["first"] = order(
                lambda q, *held: first_term(
                    [q, *parts[1:]], qkv_weight, latent, held[0] if held else None, k, block
                ),
                parts[0], *([] if state["first"] is None else [state["first"]]),
            )
            state["ends"].append(sums)
            send(("f", k), term)

        def do_final(k):
            (state["final"],) = order(
                lambda a, b, *held: final(
                    end, a, b, latent, state["mid"][1], mod, held[0] if held else None, k, block
                ),
                near["f", k], far["f", k], *([] if state["final"] is None else [state["final"]]),
            )

        def do_output(k):
            sums, state["out"] = order(
                lambda a, b, *held: output_rows(
                    end, a, b, state["feed"][0], latent, cotangent, mod, out_bias, fc2_bias,
                    held[0] if held else None, k, tokens // 2,
                ),
                near["m", k], far["m", k], *([] if state["out"] is None else [state["out"]]),
            )
            state["gate"].append(sums[0:1])

        def cast_dot(a, b):
            return dot_tn(a, b).astype(BF16)

        for k in range(chunks):
            do_attend(k)
        relay(("a", 0))
        relay(("a", 1))
        spread_out(("a", 0))
        relay(("a", 2))
        spread_out(("a", 1))
        do_feed(0)
        relay(("a", 3))
        spread_out(("a", 2))
        do_feed(1)
        spread_out(("a", 3))
        do_feed(2)
        relay(("g", 0))
        do_feed(3)
        attn_sum, normed_two, act, grad_hidden, grad_mlp = state["feed"]
        half = tokens // 2
        mlp = order(lambda a: dot(a, w_fc2).astype(BF16), act)
        relay(("g", 1))
        spread_out(("g", 0))
        send(("m", 0), mlp[:half])
        send(("m", 1), mlp[half:])
        grad_fc2 = order(cast_dot, act, grad_mlp)
        relay(("g", 2))
        spread_out(("g", 1))
        do_middle(0)
        grad_fc1 = order(cast_dot, normed_two, grad_hidden)
        grad_fc1, grad_fc2 = lax.psum((grad_fc1, grad_fc2), "dp")
        relay(("g", 3))
        spread_out(("g", 2))
        do_middle(1)
        spread_out(("g", 3))
        do_middle(2)
        do_middle(3)
        some = max(heads // 2, 1)
        parts = [*do_back(0, some)]
        relay(("m", 0))
        if heads > some:
            parts += do_back(some, heads - some)
        for k in range(chunks):
            do_first(k, parts)
        relay(("m", 1))
        spread_out(("m", 0))
        grad_out_proj = order(cast_dot, state["att"][0], state["mid"][0])
        grad_qkv = order(cast_dot, normed_one, state["first"])
        end_sums = sum(state["ends"])[0:2]
        end_parts = gather_groups(end_sums)
        relay(("f", 0))
        spread_out(("m", 1))
        do_output(0)
        relay(("f", 1))
        spread_out(("f", 0))
        do_output(1)
        output = state["out"]

        end_sums = jnp.sum(end_parts, axis=0)
        mid_sums = sum(state["middle"])
        grad_modulation = jnp.concatenate(
            [end_sums, mid_sums[2:3], mid_sums[0:2], sum(state["gate"])], axis=0
        ).reshape(1, 6 * model)
        mod_grad = lax.dynamic_slice_in_dim(grad_modulation, rank * part_width, part_width, 1)
        cond_parts = gather_groups(order(condition_term, mod_grad, w_ada))
        packed = state["first"].astype(F32)
        cond = condition.astype(F32)
        small = [
            jax.nn.silu(cond), mod_grad, sum(state["hidden"]), total(grad_mlp.astype(F32)),
            mid_sums[3:4], total(packed[:, :group]), total(packed[:, 2 * group :]),
        ]
        gathered = order(
            lambda v: lax.all_gather(v, "dp", axis=0, tiled=True), jnp.concatenate(small, axis=1)
        )
        cuts = [0]
        for v in small:
            cuts.append(cuts[-1] + v.shape[1])
        pieces = [gathered[:, a:b] for a, b in zip(cuts[:-1], cuts[1:])]
        relay(("f", 2))
        spread_out(("f", 1))
        do_final(0)
        grad_ada = order(outer, *pieces[:2])
        relay(("f", 3))
        spread_out(("f", 2))
        do_final(1)
        spread_out(("f", 3))
        do_final(2)
        grad_silu = jnp.sum(cond_parts, axis=0)
        _, silu_back = jax.vjp(jax.nn.silu, cond)
        grad_condition = silu_back(grad_silu)[0]
        grad_qkv, grad_out_proj, *_ = lax.optimization_barrier(
            (grad_qkv, grad_out_proj, grad_fc1, grad_fc2)
        )
        grad_qkv, grad_out_proj = lax.psum((grad_qkv, grad_out_proj), "dp")
        do_final(3)
        sums = [jnp.sum(v, axis=0) for v in pieces[1:]]
        return (
            output,
            state["final"],
            grad_condition,
            grad_ada,
            sums[0],
            grad_qkv.astype(F32).reshape(model, 3, group),
            jnp.stack([sums[4], sums[5]]),
            grad_out_proj.astype(F32),
            sums[3],
            grad_fc1.astype(F32),
            sums[1],
            grad_fc2.astype(F32),
            sums[2],
        )

    return local


def solution(mesh):
    rows, cols, last = P("dp", None), P(None, "mp"), P("mp")
    deep = P(None, None, "mp")
    tall = P("mp", None)
    return jax.shard_map(
        build(mesh.shape["mp"], mesh.shape["dp"]),
        mesh=mesh,
        in_specs=(
            rows, rows, P("dp"), cols, last, deep, cols, tall, P(), cols, last, tall, P(), rows,
        ),
        out_specs=(rows, rows, rows, cols, last, deep, cols, tall, P(), cols, last, tall, P()),
        check_vma=False,
    )
```

time: 720 us -> 457 us (0.63)
  waiting for transfers between devices: 455 us -> 80.7 us
  Pallas kernels: 0 us -> 121 us
  starting transfers between devices: 0.38 us -> 108 us
  matrix products: 104 us -> 20 us
  local copies, waits for them, and re-layouts: 8.92 us -> 75.6 us
  other arithmetic: 75.9 us -> 16.2 us
  blocking collectives: 56.3 us -> 10.3 us
    psum x4 -> x2, waiting for transfers between devices: 455 us -> 15.3 us  [the longest x1 15.3 us: local(): grad_qkv, grad_out_proj = lax.psum((grad_qkv, grad_out_proj), 'dp')]
    pallas_call x0 -> x56, Pallas kernels: none -> 121 us  [the longest x22 70.2 us: call(): pl.pallas_call(body, out_shape=shapes, grid_spec=pltpu.PrefetchScalarGrid...]
    ppermute x0 -> x51, starting transfers between devices: none -> 108 us  [hop(): return lax.ppermute(value, 'mp', pairs)]
    dot_general x20 -> x5, matrix products: 104 us -> 20 us  [the longest x4 15.3 us: dot_tn(): return lax.dot_general(a, b, TN, preferred_element_type=F32)]
    ppermute x0 -> x51, waiting for transfers between devices: none -> 65.4 us  [hop(): return lax.ppermute(value, 'mp', pairs)]
    unnamed x107 -> x144, local copies, waits for them, and re-layouts: 8.47 us -> 61.2 us
    reduce_sum x11 -> x7, other arithmetic: 40.6 us -> 2.34 us  [the longest x3 1.41 us: local(): sums = [jnp.sum(v, axis=0) for v in pieces[1:]]]
    psum x2 -> x0, blocking collectives: 35.2 us -> none  [the longest x1 25.3 us: local(): lax.psum(local_bias_ada.astype(jnp.bfloat16), 'dp').astype(jnp.float32)]
  transfers between devices with their start and end apart: 4 -> 53, of which waited for: 4 -> 10; matrix products, arithmetic and copies ran while one was open for 5% -> 13% of each run, Pallas kernels for 0% -> 24%
where the time goes in v1:
time: 457 us; the launch traced here: 448 us
  Pallas kernels  121 us (26%)
  starting transfers between devices  108 us (24%)
  waiting for transfers between devices  80.7 us (18%)
  local copies, waits for them, and re-layouts  75.6 us (17%)
  matrix products  20 us (4%)
  other arithmetic  16.2 us (4%)
  between operations  16.2 us (4%)
  blocking collectives  10.3 us (2%)
    ppermute x51, starting transfers between devices, hop(): return lax.ppermute(value, 'mp', pairs)  108 us
    pallas_call x22, Pallas kernels, call(): pl.pallas_call(body, out_shape=shapes, grid_spec=pltpu.PrefetchScalarGrid...  70.2 us
    ppermute x51, waiting for transfers between devices, hop(): return lax.ppermute(value, 'mp', pairs)  65.4 us
    unnamed x144, local copies, waits for them, and re-layouts  61.2 us
    pallas_call x28, Pallas kernels, add(): pl.pallas_call(add_kernel, out_shape=jax.ShapeDtypeStruct(a.shape, BF16),...  24.8 us
    pallas_call x2, Pallas kernels, attend_back(): pl.pallas_call(attend_back_body, out_shape=[full((tokens, width), BF16)]...  16.2 us
    psum x1, waiting for transfers between devices, local(): grad_qkv, grad_out_proj = lax.psum((grad_qkv, grad_out_proj), 'dp')  15.3 us
    dot_general x4, matrix products, dot_tn(): return lax.dot_general(a, b, TN, preferred_element_type=F32)  15.3 us
  transfers between devices with their start and end apart: 53, of which 10 were waited for; matrix products, arithmetic and copies ran while one was open for 13% of the time, Pallas kernels for 24%

profile of v1, /device:TPU:0, one launch (start us, length us, event | category | flops | bytes accessed | tf_op | source)
XLA Modules:
  0.0 448.1 jit_solution(7457065295476753163)
XLA Ops:
  7.2 6.4 %copy.87.w_ref = bf16[1152,1728]{1,0:T(8,128)(2,1)} copy(bf16[1152,1728]{0,1:T(8,128)(2,1)} %param.17) | data formatting | bytes 7962624 | tf_op args[3]
  16.8 5.1 %collective-permute-start = (f32[1,1728]{1,0:T(1,128)S(1)}, f32[1,1728]{1,0:T(1,128)S(1)}, u32[]{:S(2)}, u32[]{:S(2)}) collective-permute-start(f32[1,1728]{1,0:T(1,128)S(1)} %modulate.1), channel_id=1, source_target_pairs={{0,3},{1,0},{2,1},{3,2},{4,7},{5,4},{6,5},{7,6},{8,11},{9,8},{10,9... | collective-permute-start | bytes 20744 | tf_op jit(solution)/shard_map/ppermute | solution.py:531
  23.0 4.1 copy.88.w_ref.refs_6_
  29.6 5.5 %project.1 = (bf16[1024,1152]{1,0:T(8,128)(2,1)S(1)}, bf16[1024,512]{1,0:T(8,128)(2,1)S(1)}, bf16[1024,512]{1,0:T(8,128)(2,1)S(1)}, bf16[1024,512]{1,0:T(8,128)(2,1)S(1)}) custom-call(s32[1]{0:T(128)S(6)} %copy.150.len_ref, bf16[1024,1152]{1,0:T(8,128)(2,1)S(1)} %copy-done, f32[8,1152]{1,0:T(8,128)S(1)} %pad.4.mod_ref.refs_5_.refs_6_, ...), custom_call_target="tpu_custom_call" | custom-call | flops 3623878656 | bytes 9437184 | tf_op jit(solution)/shard_map/project/pallas_call | solution.py:235
  36.5 2.7 attend.4
  39.2 4.4 collective-permute-start.4
  43.6 2.7 attend.5
  47.9 2.7 attend.6
  50.7 3.6 attend.7
  54.3 3.1 collective-permute-done.4.b_ref
  58.2 6.5 %collective-permute-start.9 = (bf16[256,1152]{1,0:T(8,128)(2,1)S(1)}, bf16[256,1152]{1,0:T(8,128)(2,1)}, u32[]{:S(2)}, u32[]{:S(2)}) collective-permute-start(bf16[256,1152]{1,0:T(8,128)(2,1)S(1)} %get-tuple-element.285.a_ref), channel_id=1, source_target_pairs={{0,1},{3,2},{4,5},{7,6},{8,9},{11,10},{12,13},{15,14},{16,17},{19,... | collective-permute-start | bytes 1769480 | tf_op jit(solution)/shard_map/ppermute | solution.py:531
  64.7 5.3 %collective-permute-done.6.b_ref = bf16[256,1152]{1,0:T(8,128)(2,1)S(1)} collective-permute-done((bf16[256,1152]{1,0:T(8,128)(2,1)S(1)}, bf16[256,1152]{1,0:T(8,128)(2,1)S(1)}, u32[]{:S(2)}, u32[]{:S(2)}) %collective-permute-start.6) | collective-permute-done | bytes 589856 | tf_op jit(solution)/shard_map/ppermute | solution.py:531
  73.9 5.7 %collective-permute-start.3 = (bf16[256,1152]{1,0:T(8,128)(2,1)}, bf16[256,1152]{1,0:T(8,128)(2,1)}, u32[]{:S(2)}, u32[]{:S(2)}) collective-permute-start(bf16[256,1152]{1,0:T(8,128)(2,1)} %get-tuple-element.292.a_ref), channel_id=1, source_target_pairs={{0,1},{3,2},{4,5},{7,6},{8,9},{11,10},{12,13},{15,14},{16,17},{19,... | collective-permute-start | bytes 1769480 | tf_op jit(solution)/shard_map/ppermute | solution.py:531
  79.7 3.0 collective-permute-done.9.b_ref
  89.2 6.2 %feed.4 = (bf16[256,1152]{1,0:T(8,128)(2,1)S(1)}, f32[8,1152]{1,0:T(8,128)S(1)}, bf16[1024,1152]{1,0:T(8,128)(2,1)S(1)}, bf16[1024,1152]{1,0:T(8,128)(2,1)S(1)},...) custom-call(s32[1]{0:T(128)} %bitcast.refs_0_, ...), custom_call_target="tpu_custom_call" | custom-call | flops 2038431744 | bytes 8847360 | tf_op jit(solution)/shard_map/feed/pallas_call | solution.py:97
  98.9 9.4 %collective-permute-start.15 = (bf16[256,1152]{1,0:T(8,128)(2,1)S(1)}, bf16[256,1152]{1,0:T(8,128)(2,1)S(1)}, u32[]{:S(2)}, u32[]{:S(2)}) collective-permute-start(bf16[256,1152]{1,0:T(8,128)(2,1)S(1)} %get-tuple-element.329.a_ref), channel_id=1, source_target_pairs={{0,1},{3,2},{4,5},{7,6},{8,9},{11,10},{12,13},{15,14},{16,17},{19,... | collective-permute-start | bytes 1769480 | tf_op jit(solution)/shard_map/ppermute | solution.py:531
  108.4 6.2 %feed.5 = (bf16[256,1152]{1,0:T(8,128)(2,1)S(1)}, f32[8,1152]{1,0:T(8,128)S(1)}, bf16[1024,1152]{1,0:T(8,128)(2,1)S(1)}, bf16[1024,1152]{1,0:T(8,128)(2,1)S(1)},...) custom-call(s32[1]{0:T(128)} %bitcast.refs_0_, ...), custom_call_target="tpu_custom_call", output_to_operand_aliasing={{2}: (10, {}), {3}: (11, {}), {4}: (12, {}), {5}: (13, {}),... | custom-call | flops 2038431744 | bytes 8847360 | tf_op jit(solution)/shard_map/feed/pallas_call | solution.py:97
  116.1 4.6 %collective-permute-start.19 = (bf16[256,1152]{1,0:T(8,128)(2,1)S(1)}, bf16[256,1152]{1,0:T(8,128)(2,1)S(1)}, u32[]{:S(2)}, u32[]{:S(2)}) collective-permute-start(bf16[256,1152]{1,0:T(8,128)(2,1)S(1)} %get-tuple-element.343.a_ref), channel_id=1, source_target_pairs={{0,1},{3,2},{4,5},{7,6},{8,9},{11,10},{12,13},{15,14},{16,17},{19,... | collective-permute-start | bytes 1769480 | tf_op jit(solution)/shard_map/ppermute | solution.py:531
  120.7 6.2 %feed.6 = (bf16[256,1152]{1,0:T(8,128)(2,1)S(1)}, f32[8,1152]{1,0:T(8,128)S(1)}, bf16[1024,1152]{1,0:T(8,128)(2,1)S(1)}, bf16[1024,1152]{1,0:T(8,128)(2,1)S(1)},...) custom-call(s32[1]{0:T(128)} %bitcast.refs_0_, ...), custom_call_target="tpu_custom_call", output_to_operand_aliasing={{2}: (10, {}), {3}: (11, {}), {4}: (12, {}), {5}: (13, {}),... | custom-call | flops 2038431744 | bytes 8847360 | tf_op jit(solution)/shard_map/feed/pallas_call | solution.py:97
  129.1 7.1 %feed.7 = (bf16[256,1152]{1,0:T(8,128)(2,1)}, f32[8,1152]{1,0:T(8,128)S(1)}, bf16[1024,1152]{1,0:T(8,128)(2,1)S(1)}, bf16[1024,1152]{1,0:T(8,128)(2,1)S(1)}, bf1...) custom-call(s32[1]{0:T(128)} %bitcast.refs_0_, ...), custom_call_target="tpu_custom_call", output_to_operand_aliasing={{2}: (10, {}), {3}: (11, {}), {4}: (12, {}), {5}: (13, {}),... | custom-call | flops 2038431744 | bytes 8847360 | tf_op jit(solution)/shard_map/feed/pallas_call | solution.py:97
  136.3 3.3 collective-permute-start.17
  139.6 4.7 %convolution_convert_fusion.2 = bf16[1024,1152]{1,0:T(8,128)(2,1)} fusion(bf16[1024,1152]{1,0:T(8,128)(2,1)S(1)} %get-tuple-element.348, bf16[1152,1152]{1,0:T(8,128)(2,1)S(1)} %copy-done.54), kind=kOutput, calls=%fused_computation.3 | convolution fusion | flops 2719088640 | bytes 7372800 | tf_op jit(solution)/shard_map/dot_general | solution.py:29
  146.8 4.8 %convolution_convert_fusion.1 = bf16[1152,1152]{1,0:T(8,128)(2,1)} fusion(bf16[1024,1152]{1,0:T(8,128)(2,1)S(1)} %get-tuple-element.348, bf16[1024,1152]{1,0:T(8,128)(2,1)S(1)} %get-tuple-element.349), kind=kOutput, calls=%fused_computation.1 | convolution fusion | flops 2719236096 | bytes 7372800 | tf_op jit(solution)/shard_map/dot_general | solution.py:37
  164.9 4.8 %convolution_convert_fusion = bf16[1152,1152]{1,0:T(8,128)(2,1)} fusion(bf16[1024,1152]{1,0:T(8,128)(2,1)S(1)} %get-tuple-element.358, bf16[1024,1152]{1,0:T(8,128)(2,1)S(1)} %get-tuple-element.359), kind=kOutput, calls=%fused_computation | convolution fusion | flops 2719236096 | bytes 7372800 | tf_op jit(solution)/shard_map/dot_general | solution.py:37
  173.5 3.3 fusion.2
  176.8 7.1 %collective-permute-start.28 = (bf16[512,1152]{1,0:T(8,128)(2,1)}, bf16[512,1152]{1,0:T(8,128)(2,1)}, u32[]{:S(2)}, u32[]{:S(2)}) collective-permute-start(bf16[512,1152]{1,0:T(8,128)(2,1)} %get-tuple-element.398.a_ref), channel_id=1, source_target_pairs={{0,1},{3,2},{4,5},{7,6},{8,9},{11,10},{12,13},{15,14},{16,17},{19,... | collective-permute-start | bytes 3538952 | tf_op jit(solution)/shard_map/ppermute | solution.py:531
  194.9 3.1 middle.5
  205.9 7.2 %collective-permute-start.16 = (bf16[512,1152]{1,0:T(8,128)(2,1)}, bf16[512,1152]{1,0:T(8,128)(2,1)}, u32[]{:S(2)}, u32[]{:S(2)}) collective-permute-start(bf16[512,1152]{1,0:T(8,128)(2,1)} %get-tuple-element.420.a_ref), channel_id=1, source_target_pairs={{0,1},{3,2},{4,5},{7,6},{8,9},{11,10},{12,13},{15,14},{16,17},{19,... | collective-permute-start | bytes 3538952 | tf_op jit(solution)/shard_map/ppermute | solution.py:531
  222.3 3.0 middle.6
  225.4 3.1 middle.7
  233.0 8.1 %attend_back.2 = (bf16[1024,256]{1,0:T(8,128)(2,1)S(1)}, bf16[1024,256]{1,0:T(8,128)(2,1)S(1)}, bf16[1024,256]{1,0:T(8,128)(2,1)S(1)}) custom-call(bf16[1024,512]{1,0:T(8,128)(2,1)S(1)} %copy-done.32, bf16[1024,512]{1,0:T(8,128)(2,1)S(1)} %copy-done.34, bf16[1024,512]{1,0:T(8,128)(2,1)S(1)} %copy-done.36, bf16[1024,512]{1,0:T(8,128)(2,1)S(1)} %copy-done.46, ...), custom_call_target="tpu_custom_call" | custom-call | flops 2684354560 | bytes 4718592 | tf_op jit(solution)/shard_map/attend_back/pallas_call | solution.py:416
  243.0 8.1 %attend_back.3 = (bf16[1024,256]{1,0:T(8,128)(2,1)S(1)}, bf16[1024,256]{1,0:T(8,128)(2,1)S(1)}, bf16[1024,256]{1,0:T(8,128)(2,1)S(1)}) custom-call(bf16[1024,512]{1,0:T(8,128)(2,1)S(1)} %copy-done.32, bf16[1024,512]{1,0:T(8,128)(2,1)S(1)} %copy-done.34, bf16[1024,512]{1,0:T(8,128)(2,1)S(1)} %copy-done.36, bf16[1024,512]{1,0:T(8,128)(2,1)S(1)} %copy-done.46, ...), custom_call_target="tpu_custom_call" | custom-call | flops 2684354560 | bytes 4718592 | tf_op jit(solution)/shard_map/attend_back/pallas_call | solution.py:416
  258.3 3.5 collective-permute-start.37
  263.4 6.0 %collective-permute-start.30 = (bf16[256,1152]{1,0:T(8,128)(2,1)S(1)}, bf16[256,1152]{1,0:T(8,128)(2,1)S(1)}, u32[]{:S(2)}, u32[]{:S(2)}) collective-permute-start(bf16[256,1152]{1,0:T(8,128)(2,1)S(1)} %get-tuple-element.431.a_ref), channel_id=1, source_target_pairs={{0,1},{3,2},{4,5},{7,6},{8,9},{11,10},{12,13},{15,14},{16,17},{19,... | collective-permute-start | bytes 1769480 | tf_op jit(solution)/shard_map/ppermute | solution.py:531
  281.6 3.8 convolution_convert_fusion.3
  288.2 31.2 %collective-permute-done.33.refs_2_ = bf16[512,1152]{1,0:T(8,128)(2,1)S(1)} collective-permute-done((bf16[512,1152]{1,0:T(8,128)(2,1)S(1)}, bf16[512,1152]{1,0:T(8,128)(2,1)S(1)}, u32[]{:S(2)}, u32[]{:S(2)}) %collective-permute-start.33) | collective-permute-done | bytes 1179680 | tf_op jit(solution)/shard_map/ppermute | solution.py:531
  324.3 13.1 %collective-permute-done.32.refs_2_ = bf16[512,1152]{1,0:T(8,128)(2,1)S(1)} collective-permute-done((bf16[512,1152]{1,0:T(8,128)(2,1)S(1)}, bf16[512,1152]{1,0:T(8,128)(2,1)S(1)}, u32[]{:S(2)}, u32[]{:S(2)}) %collective-permute-start.32) | collective-permute-done | bytes 1179680 | tf_op jit(solution)/shard_map/ppermute | solution.py:531
  339.7 6.4 %copy.93.w_ref = bf16[1152,1728]{1,0:T(8,128)(2,1)} copy(bf16[1152,1728]{0,1:T(8,128)(2,1)} %param.17) | data formatting | bytes 7962624 | tf_op jit(solution)/shard_map/optimization_barrier | solution.py:521
  357.4 10.3 %all-gather = f32[8,1,6912]{2,1,0:T(1,128)S(1)} all-gather(f32[1,1,6912]{2,1,0:T(1,128)S(1)} %bitcast.54), channel_id=1, replica_groups=mesh['dp'=8,'mp'=4] {'dp'}, dimensions={0}, use_global_device_ids=true | all-gather | bytes 248832 | tf_op jit(solution)/shard_map/all_gather | solution.py:729
  376.3 2.8 final.4.refs_6_
  380.7 3.3 copy-done.28
  387.6 5.9 %collective-permute-done.44.refs_2_ = bf16[256,1152]{1,0:T(8,128)(2,1)S(1)} collective-permute-done((bf16[256,1152]{1,0:T(8,128)(2,1)S(1)}, bf16[256,1152]{1,0:T(8,128)(2,1)S(1)}, u32[]{:S(2)}, u32[]{:S(2)}) %collective-permute-start.44) | collective-permute-done | bytes 589856 | tf_op jit(solution)/shard_map/ppermute | solution.py:531
  397.8 2.7 convert_element_type.53
  403.9 15.3 %all-reduce.6.cloned.1.call-done = (bf16[1152,3,288]{0,2,1:T(8,128)(2,1)}, bf16[288,1152]{1,0:T(8,128)(2,1)}) async-done(((bf16[1152,3,288]{0,2,1:T(8,128)(2,1)}, bf16[288,1152]{1,0:T(8,128)(2,1)}), (bf16[1152,3,288]{0,2,1:T(8,128)(2,1)}, bf16[288,1152]{1,0:T(8,128)(2,1)})) %all-reduce.6.cloned.1.call-update) | async-done | bytes 2654224 | tf_op jit(solution)/shard_map/psum | solution.py:750
  419.2 3.8 reshape.82
  424.2 8.8 %copy.94 = f32[1152,1728]{0,1:T(8,128)} copy(f32[1152,1728]{1,0:T(8,128)} %copy-done.28) | data formatting | bytes 15925248
  435.3 2.8 final.6.refs_6_
  438.1 3.0 final.7
  (315 shorter events, 148.1 us)
Async XLA Ops:
  7.2 345.2 %all-reduce.8.cloned.1.call-start = ((), (), s32[]{:S(2)}) async-start(), calls=%async_computation.1 | async-start | bytes 10616832 | tf_op jit(solution)/shard_map/psum | solution.py:687
  16.8 11.0 %collective-permute-start = (f32[1,1728]{1,0:T(1,128)S(1)}, f32[1,1728]{1,0:T(1,128)S(1)}, u32[]{:S(2)}, u32[]{:S(2)}) collective-permute-start(f32[1,1728]{1,0:T(1,128)S(1)} %modulate.1), channel_id=1, source_target_pairs={{0,3},{1,0},{2,1},{3,2},{4,7},{5,4},{6,5},{7,6},{8,11},{9,8},{10,9... | collective-permute-start | bytes 20744 | tf_op jit(solution)/shard_map/ppermute | solution.py:531
  39.2 18.1 %collective-permute-start.4 = (bf16[256,1152]{1,0:T(8,128)(2,1)S(1)}, bf16[256,1152]{1,0:T(8,128)(2,1)S(1)}, u32[]{:S(2)}, u32[]{:S(2)}) collective-permute-start(bf16[256,1152]{1,0:T(8,128)(2,1)S(1)} %get-tuple-element.279.a_ref), channel_id=1, source_target_pairs={{0,1},{3,2},{4,5},{7,6},{8,9},{11,10},{12,13},{15,14},{16,17},{19,... | collective-permute-start | bytes 1769480 | tf_op jit(solution)/shard_map/ppermute | solution.py:531
  46.4 23.6 %collective-permute-start.6 = (bf16[256,1152]{1,0:T(8,128)(2,1)S(1)}, bf16[256,1152]{1,0:T(8,128)(2,1)S(1)}, u32[]{:S(2)}, u32[]{:S(2)}) collective-permute-start(bf16[256,1152]{1,0:T(8,128)(2,1)S(1)} %get-tuple-element.281.a_ref), channel_id=1, source_target_pairs={{0,1},{3,2},{4,5},{7,6},{8,9},{11,10},{12,13},{15,14},{16,17},{19,... | collective-permute-start | bytes 1769480 | tf_op jit(solution)/shard_map/ppermute | solution.py:531
  57.5 14.9 %collective-permute-start.5 = (bf16[256,1152]{1,0:T(8,128)(2,1)S(1)}, bf16[256,1152]{1,0:T(8,128)(2,1)S(1)}, u32[]{:S(2)}, u32[]{:S(2)}) collective-permute-start(bf16[256,1152]{1,0:T(8,128)(2,1)S(1)} %add.125.a_ref), channel_id=1, source_target_pairs={{1,2},{2,1},{5,6},{6,5},{9,10},{10,9},{13,14},{14,13},{17,18},{18,... | collective-permute-start | bytes 1769480 | tf_op jit(solution)/shard_map/ppermute | solution.py:531
  58.2 24.4 %collective-permute-start.9 = (bf16[256,1152]{1,0:T(8,128)(2,1)S(1)}, bf16[256,1152]{1,0:T(8,128)(2,1)}, u32[]{:S(2)}, u32[]{:S(2)}) collective-permute-start(bf16[256,1152]{1,0:T(8,128)(2,1)S(1)} %get-tuple-element.285.a_ref), channel_id=1, source_target_pairs={{0,1},{3,2},{4,5},{7,6},{8,9},{11,10},{12,13},{15,14},{16,17},{19,... | collective-permute-start | bytes 1769480 | tf_op jit(solution)/shard_map/ppermute | solution.py:531
  71.0 13.6 %collective-permute-start.8 = (bf16[256,1152]{1,0:T(8,128)(2,1)}, bf16[256,1152]{1,0:T(8,128)(2,1)}, u32[]{:S(2)}, u32[]{:S(2)}) collective-permute-start(bf16[256,1152]{1,0:T(8,128)(2,1)} %add.126.a_ref), channel_id=1, source_target_pairs={{1,2},{2,1},{5,6},{6,5},{9,10},{10,9},{13,14},{14,13},{17,18},{18,... | collective-permute-start | bytes 1769480 | tf_op jit(solution)/shard_map/ppermute | solution.py:531
  72.6 14.7 %collective-permute-start.7 = (bf16[256,1152]{1,0:T(8,128)(2,1)S(1)}, bf16[256,1152]{1,0:T(8,128)(2,1)S(1)}, u32[]{:S(2)}, u32[]{:S(2)}) collective-permute-start(bf16[256,1152]{1,0:T(8,128)(2,1)S(1)} %add.127.refs_1_), channel_id=1, source_target_pairs={{1,0},{2,3},{5,4},{6,7},{9,8},{10,11},{13,12},{14,15},{17,16},{18,... | collective-permute-start | bytes 1769480 | tf_op jit(solution)/shard_map/ppermute | solution.py:531
  73.9 21.5 %collective-permute-start.3 = (bf16[256,1152]{1,0:T(8,128)(2,1)}, bf16[256,1152]{1,0:T(8,128)(2,1)}, u32[]{:S(2)}, u32[]{:S(2)}) collective-permute-start(bf16[256,1152]{1,0:T(8,128)(2,1)} %get-tuple-element.292.a_ref), channel_id=1, source_target_pairs={{0,1},{3,2},{4,5},{7,6},{8,9},{11,10},{12,13},{15,14},{16,17},{19,... | collective-permute-start | bytes 1769480 | tf_op jit(solution)/shard_map/ppermute | solution.py:531
  83.9 13.6 %collective-permute-start.12 = (bf16[256,1152]{1,0:T(8,128)(2,1)S(1)}, bf16[256,1152]{1,0:T(8,128)(2,1)S(1)}, u32[]{:S(2)}, u32[]{:S(2)}) collective-permute-start(bf16[256,1152]{1,0:T(8,128)(2,1)S(1)} %add.128.a_ref), channel_id=1, source_target_pairs={{1,2},{2,1},{5,6},{6,5},{9,10},{10,9},{13,14},{14,13},{17,18},{18,... | collective-permute-start | bytes 1769480 | tf_op jit(solution)/shard_map/ppermute | solution.py:531
  86.0 22.4 %collective-permute-start.11 = (bf16[256,1152]{1,0:T(8,128)(2,1)S(1)}, bf16[256,1152]{1,0:T(8,128)(2,1)S(1)}, u32[]{:S(2)}, u32[]{:S(2)}) collective-permute-start(bf16[256,1152]{1,0:T(8,128)(2,1)S(1)} %add.129.refs_1_), channel_id=1, source_target_pairs={{1,0},{2,3},{5,4},{6,7},{9,8},{10,11},{13,12},{14,15},{17,16},{18,... | collective-permute-start | bytes 1769480 | tf_op jit(solution)/shard_map/ppermute | solution.py:531
  96.8 17.8 %collective-permute-start.10 = (bf16[256,1152]{1,0:T(8,128)(2,1)S(1)}, bf16[256,1152]{1,0:T(8,128)(2,1)S(1)}, u32[]{:S(2)}, u32[]{:S(2)}) collective-permute-start(bf16[256,1152]{1,0:T(8,128)(2,1)S(1)} %add.130.a_ref), channel_id=1, source_target_pairs={{1,2},{2,1},{5,6},{6,5},{9,10},{10,9},{13,14},{14,13},{17,18},{18,... | collective-permute-start | bytes 1769480 | tf_op jit(solution)/shard_map/ppermute | solution.py:531
  97.6 23.1 %collective-permute-start.14 = (bf16[256,1152]{1,0:T(8,128)(2,1)S(1)}, bf16[256,1152]{1,0:T(8,128)(2,1)S(1)}, u32[]{:S(2)}, u32[]{:S(2)}) collective-permute-start(bf16[256,1152]{1,0:T(8,128)(2,1)S(1)} %add.131.refs_1_), channel_id=1, source_target_pairs={{1,0},{2,3},{5,4},{6,7},{9,8},{10,11},{13,12},{14,15},{17,16},{18,... | collective-permute-start | bytes 1769480 | tf_op jit(solution)/shard_map/ppermute | solution.py:531
  98.9 29.3 %collective-permute-start.15 = (bf16[256,1152]{1,0:T(8,128)(2,1)S(1)}, bf16[256,1152]{1,0:T(8,128)(2,1)S(1)}, u32[]{:S(2)}, u32[]{:S(2)}) collective-permute-start(bf16[256,1152]{1,0:T(8,128)(2,1)S(1)} %get-tuple-element.329.a_ref), channel_id=1, source_target_pairs={{0,1},{3,2},{4,5},{7,6},{8,9},{11,10},{12,13},{15,14},{16,17},{19,... | collective-permute-start | bytes 1769480 | tf_op jit(solution)/shard_map/ppermute | solution.py:531
  114.8 14.3 %collective-permute-start.13 = (bf16[256,1152]{1,0:T(8,128)(2,1)S(1)}, bf16[256,1152]{1,0:T(8,128)(2,1)S(1)}, u32[]{:S(2)}, u32[]{:S(2)}) collective-permute-start(bf16[256,1152]{1,0:T(8,128)(2,1)S(1)} %add.132.refs_1_), channel_id=1, source_target_pairs={{1,0},{2,3},{5,4},{6,7},{9,8},{10,11},{13,12},{14,15},{17,16},{18,... | collective-permute-start | bytes 1769480 | tf_op jit(solution)/shard_map/ppermute | solution.py:531
  116.1 28.2 %collective-permute-start.19 = (bf16[256,1152]{1,0:T(8,128)(2,1)S(1)}, bf16[256,1152]{1,0:T(8,128)(2,1)S(1)}, u32[]{:S(2)}, u32[]{:S(2)}) collective-permute-start(bf16[256,1152]{1,0:T(8,128)(2,1)S(1)} %get-tuple-element.343.a_ref), channel_id=1, source_target_pairs={{0,1},{3,2},{4,5},{7,6},{8,9},{11,10},{12,13},{15,14},{16,17},{19,... | collective-permute-start | bytes 1769480 | tf_op jit(solution)/shard_map/ppermute | solution.py:531
  126.9 24.7 %collective-permute-start.22 = (bf16[256,1152]{1,0:T(8,128)(2,1)S(1)}, bf16[256,1152]{1,0:T(8,128)(2,1)S(1)}, u32[]{:S(2)}, u32[]{:S(2)}) collective-permute-start(bf16[256,1152]{1,0:T(8,128)(2,1)S(1)} %get-tuple-element.350.a_ref), channel_id=1, source_target_pairs={{0,1},{3,2},{4,5},{7,6},{8,9},{11,10},{12,13},{15,14},{16,17},{19,... | collective-permute-start | bytes 1769480 | tf_op jit(solution)/shard_map/ppermute | solution.py:531
  128.4 16.9 %collective-permute-start.18 = (bf16[256,1152]{1,0:T(8,128)(2,1)S(1)}, bf16[256,1152]{1,0:T(8,128)(2,1)S(1)}, u32[]{:S(2)}, u32[]{:S(2)}) collective-permute-start(bf16[256,1152]{1,0:T(8,128)(2,1)S(1)} %add.133.a_ref), channel_id=1, source_target_pairs={{1,2},{2,1},{5,6},{6,5},{9,10},{10,9},{13,14},{14,13},{17,18},{18,... | collective-permute-start | bytes 1769480 | tf_op jit(solution)/shard_map/ppermute | solution.py:531
  136.3 33.4 %collective-permute-start.17 = (bf16[256,1152]{1,0:T(8,128)(2,1)}, bf16[256,1152]{1,0:T(8,128)(2,1)}, u32[]{:S(2)}, u32[]{:S(2)}) collective-permute-start(bf16[256,1152]{1,0:T(8,128)(2,1)} %get-tuple-element.360.a_ref), channel_id=1, source_target_pairs={{0,1},{3,2},{4,5},{7,6},{8,9},{11,10},{12,13},{15,14},{16,17},{19,... | collective-permute-start | bytes 1769480 | tf_op jit(solution)/shard_map/ppermute | solution.py:531
  144.4 9.6 %collective-permute-start.21 = (bf16[256,1152]{1,0:T(8,128)(2,1)S(1)}, bf16[256,1152]{1,0:T(8,128)(2,1)S(1)}, u32[]{:S(2)}, u32[]{:S(2)}) collective-permute-start(bf16[256,1152]{1,0:T(8,128)(2,1)S(1)} %add.134.a_ref), channel_id=1, source_target_pairs={{1,2},{2,1},{5,6},{6,5},{9,10},{10,9},{13,14},{14,13},{17,18},{18,... | collective-permute-start | bytes 1769480 | tf_op jit(solution)/shard_map/ppermute | solution.py:531
  145.4 13.1 %collective-permute-start.20 = (bf16[256,1152]{1,0:T(8,128)(2,1)S(1)}, bf16[256,1152]{1,0:T(8,128)(2,1)S(1)}, u32[]{:S(2)}, u32[]{:S(2)}) collective-permute-start(bf16[256,1152]{1,0:T(8,128)(2,1)S(1)} %add.135.refs_1_), channel_id=1, source_target_pairs={{1,0},{2,3},{5,4},{6,7},{9,8},{10,11},{13,12},{14,15},{17,16},{18,... | collective-permute-start | bytes 1769480 | tf_op jit(solution)/shard_map/ppermute | solution.py:531
  152.6 31.4 %collective-permute-start.25 = (bf16[256,1152]{1,0:T(8,128)(2,1)}, bf16[256,1152]{1,0:T(8,128)(2,1)}, u32[]{:S(2)}, u32[]{:S(2)}) collective-permute-start(bf16[256,1152]{1,0:T(8,128)(2,1)} %add.136.a_ref), channel_id=1, source_target_pairs={{1,2},{2,1},{5,6},{6,5},{9,10},{10,9},{13,14},{14,13},{17,18},{18,... | collective-permute-start | bytes 1769480 | tf_op jit(solution)/shard_map/ppermute | solution.py:531
  155.0 32.5 %collective-permute-start.24 = (bf16[256,1152]{1,0:T(8,128)(2,1)}, bf16[256,1152]{1,0:T(8,128)(2,1)}, u32[]{:S(2)}, u32[]{:S(2)}) collective-permute-start(bf16[256,1152]{1,0:T(8,128)(2,1)} %add.137.refs_1_), channel_id=1, source_target_pairs={{1,0},{2,3},{5,4},{6,7},{9,8},{10,11},{13,12},{14,15},{17,16},{18,... | collective-permute-start | bytes 1769480 | tf_op jit(solution)/shard_map/ppermute | solution.py:531
  171.9 29.7 %collective-permute-start.23 = (bf16[256,1152]{1,0:T(8,128)(2,1)}, bf16[256,1152]{1,0:T(8,128)(2,1)}, u32[]{:S(2)}, u32[]{:S(2)}) collective-permute-start(bf16[256,1152]{1,0:T(8,128)(2,1)} %add.138.a_ref), channel_id=1, source_target_pairs={{1,2},{2,1},{5,6},{6,5},{9,10},{10,9},{13,14},{14,13},{17,18},{18,... | collective-permute-start | bytes 1769480 | tf_op jit(solution)/shard_map/ppermute | solution.py:531
  176.8 64.3 %collective-permute-start.28 = (bf16[512,1152]{1,0:T(8,128)(2,1)}, bf16[512,1152]{1,0:T(8,128)(2,1)}, u32[]{:S(2)}, u32[]{:S(2)}) collective-permute-start(bf16[512,1152]{1,0:T(8,128)(2,1)} %get-tuple-element.398.a_ref), channel_id=1, source_target_pairs={{0,1},{3,2},{4,5},{7,6},{8,9},{11,10},{12,13},{15,14},{16,17},{19,... | collective-permute-start | bytes 3538952 | tf_op jit(solution)/shard_map/ppermute | solution.py:531
  186.2 27.3 %collective-permute-start.27 = (bf16[256,1152]{1,0:T(8,128)(2,1)}, bf16[256,1152]{1,0:T(8,128)(2,1)}, u32[]{:S(2)}, u32[]{:S(2)}) collective-permute-start(bf16[256,1152]{1,0:T(8,128)(2,1)} %add.139.refs_1_), channel_id=1, source_target_pairs={{1,0},{2,3},{5,4},{6,7},{9,8},{10,11},{13,12},{14,15},{17,16},{18,... | collective-permute-start | bytes 1769480 | tf_op jit(solution)/shard_map/ppermute | solution.py:531
  204.2 21.1 %collective-permute-start.26 = (bf16[256,1152]{1,0:T(8,128)(2,1)}, bf16[256,1152]{1,0:T(8,128)(2,1)}, u32[]{:S(2)}, u32[]{:S(2)}) collective-permute-start(bf16[256,1152]{1,0:T(8,128)(2,1)} %add.140.refs_1_), channel_id=1, source_target_pairs={{1,0},{2,3},{5,4},{6,7},{9,8},{10,11},{13,12},{14,15},{17,16},{18,... | collective-permute-start | bytes 1769480 | tf_op jit(solution)/shard_map/ppermute | solution.py:531
  205.9 57.5 %collective-permute-start.16 = (bf16[512,1152]{1,0:T(8,128)(2,1)}, bf16[512,1152]{1,0:T(8,128)(2,1)}, u32[]{:S(2)}, u32[]{:S(2)}) collective-permute-start(bf16[512,1152]{1,0:T(8,128)(2,1)} %get-tuple-element.420.a_ref), channel_id=1, source_target_pairs={{0,1},{3,2},{4,5},{7,6},{8,9},{11,10},{12,13},{15,14},{16,17},{19,... | collective-permute-start | bytes 3538952 | tf_op jit(solution)/shard_map/ppermute | solution.py:531
  213.1 206.2 %all-reduce.6.cloned.1.call-start = ((), (), s32[]{:S(2)}) async-start(), calls=%async_computation | async-start | bytes 5308416 | tf_op jit(solution)/shard_map/psum | solution.py:750
  258.3 15.1 %collective-permute-start.37 = (f32[2,1152]{1,0:T(2,128)S(1)}, f32[2,1152]{1,0:T(2,128)S(1)}, u32[]{:S(2)}, u32[]{:S(2)}) collective-permute-start(f32[2,1152]{1,0:T(2,128)S(1)} %get-tuple-element.553), channel_id=1, source_target_pairs={{0,3},{1,0},{2,1},{3,2},{4,7},{5,4},{6,5},{7,6},{8,11},{9,8},{10,9... | collective-permute-start | bytes 27656 | tf_op jit(solution)/shard_map/ppermute | solution.py:531
  261.8 13.3 %collective-permute-start.38 = (f32[2,1152]{1,0:T(2,128)S(1)}, f32[2,1152]{1,0:T(2,128)S(1)}, u32[]{:S(2)}, u32[]{:S(2)}) collective-permute-start(f32[2,1152]{1,0:T(2,128)S(1)} %get-tuple-element.553), channel_id=1, source_target_pairs={{0,2},{1,3},{2,0},{3,1},{4,6},{5,7},{6,4},{7,5},{8,10},{9,11},{10,... | collective-permute-start | bytes 27656 | tf_op jit(solution)/shard_map/ppermute | solution.py:531
  261.8 15.5 %collective-permute-start.39 = (f32[2,1152]{1,0:T(2,128)S(1)}, f32[2,1152]{1,0:T(2,128)S(1)}, u32[]{:S(2)}, u32[]{:S(2)}) collective-permute-start(f32[2,1152]{1,0:T(2,128)S(1)} %get-tuple-element.553), channel_id=1, source_target_pairs={{0,1},{1,2},{2,3},{3,0},{4,5},{5,6},{6,7},{7,4},{8,9},{9,10},{10,1... | collective-permute-start | bytes 27656 | tf_op jit(solution)/shard_map/ppermute | solution.py:531
  262.5 15.6 %collective-permute-start.31 = (bf16[512,1152]{1,0:T(8,128)(2,1)S(1)}, bf16[512,1152]{1,0:T(8,128)(2,1)S(1)}, u32[]{:S(2)}, u32[]{:S(2)}) collective-permute-start(bf16[512,1152]{1,0:T(8,128)(2,1)S(1)} %add.141.a_ref), channel_id=1, source_target_pairs={{1,2},{2,1},{5,6},{6,5},{9,10},{10,9},{13,14},{14,13},{17,18},{18,... | collective-permute-start | bytes 3538952 | tf_op jit(solution)/shard_map/ppermute | solution.py:531
  263.4 22.0 %collective-permute-start.30 = (bf16[256,1152]{1,0:T(8,128)(2,1)S(1)}, bf16[256,1152]{1,0:T(8,128)(2,1)S(1)}, u32[]{:S(2)}, u32[]{:S(2)}) collective-permute-start(bf16[256,1152]{1,0:T(8,128)(2,1)S(1)} %get-tuple-element.431.a_ref), channel_id=1, source_target_pairs={{0,1},{3,2},{4,5},{7,6},{8,9},{11,10},{12,13},{15,14},{16,17},{19,... | collective-permute-start | bytes 1769480 | tf_op jit(solution)/shard_map/ppermute | solution.py:531
  273.4 50.6 %collective-permute-start.35 = (bf16[256,1152]{1,0:T(8,128)(2,1)S(1)}, bf16[256,1152]{1,0:T(8,128)(2,1)S(1)}, u32[]{:S(2)}, u32[]{:S(2)}) collective-permute-start(bf16[256,1152]{1,0:T(8,128)(2,1)S(1)} %get-tuple-element.439.a_ref), channel_id=1, source_target_pairs={{0,1},{3,2},{4,5},{7,6},{8,9},{11,10},{12,13},{15,14},{16,17},{19,... | collective-permute-start | bytes 1769480 | tf_op jit(solution)/shard_map/ppermute | solution.py:531
  275.1 92.6 %collective-permute-start.42 = (bf16[256,1152]{1,0:T(8,128)(2,1)}, bf16[256,1152]{1,0:T(8,128)(2,1)}, u32[]{:S(2)}, u32[]{:S(2)}) collective-permute-start(bf16[256,1152]{1,0:T(8,128)(2,1)} %get-tuple-element.459.a_ref), channel_id=1, source_target_pairs={{0,1},{3,2},{4,5},{7,6},{8,9},{11,10},{12,13},{15,14},{16,17},{19,... | collective-permute-start | bytes 1769480 | tf_op jit(solution)/shard_map/ppermute | solution.py:531
  277.3 8.3 %collective-permute-start.29 = (bf16[512,1152]{1,0:T(8,128)(2,1)S(1)}, bf16[512,1152]{1,0:T(8,128)(2,1)S(1)}, u32[]{:S(2)}, u32[]{:S(2)}) collective-permute-start(bf16[512,1152]{1,0:T(8,128)(2,1)S(1)} %add.142.a_ref), channel_id=1, source_target_pairs={{1,2},{2,1},{5,6},{6,5},{9,10},{10,9},{13,14},{14,13},{17,18},{18,... | collective-permute-start | bytes 3538952 | tf_op jit(solution)/shard_map/ppermute | solution.py:531
  278.3 41.1 %collective-permute-start.33 = (bf16[512,1152]{1,0:T(8,128)(2,1)S(1)}, bf16[512,1152]{1,0:T(8,128)(2,1)S(1)}, u32[]{:S(2)}, u32[]{:S(2)}) collective-permute-start(bf16[512,1152]{1,0:T(8,128)(2,1)S(1)} %add.143.refs_1_), channel_id=1, source_target_pairs={{1,0},{2,3},{5,4},{6,7},{9,8},{10,11},{13,12},{14,15},{17,16},{18,... | collective-permute-start | bytes 3538952 | tf_op jit(solution)/shard_map/ppermute | solution.py:531
  285.9 51.5 %collective-permute-start.32 = (bf16[512,1152]{1,0:T(8,128)(2,1)S(1)}, bf16[512,1152]{1,0:T(8,128)(2,1)S(1)}, u32[]{:S(2)}, u32[]{:S(2)}) collective-permute-start(bf16[512,1152]{1,0:T(8,128)(2,1)S(1)} %add.145.refs_1_), channel_id=1, source_target_pairs={{1,0},{2,3},{5,4},{6,7},{9,8},{10,11},{13,12},{14,15},{17,16},{18,... | collective-permute-start | bytes 3538952 | tf_op jit(solution)/shard_map/ppermute | solution.py:531
  287.5 36.6 %collective-permute-start.34 = (bf16[256,1152]{1,0:T(8,128)(2,1)S(1)}, bf16[256,1152]{1,0:T(8,128)(2,1)S(1)}, u32[]{:S(2)}, u32[]{:S(2)}) collective-permute-start(bf16[256,1152]{1,0:T(8,128)(2,1)S(1)} %add.144.a_ref), channel_id=1, source_target_pairs={{1,2},{2,1},{5,6},{6,5},{9,10},{10,9},{13,14},{14,13},{17,18},{18,... | collective-permute-start | bytes 1769480 | tf_op jit(solution)/shard_map/ppermute | solution.py:531
  319.5 64.6 %collective-permute-start.36 = (bf16[256,1152]{1,0:T(8,128)(2,1)}, bf16[256,1152]{1,0:T(8,128)(2,1)}, u32[]{:S(2)}, u32[]{:S(2)}) collective-permute-start(bf16[256,1152]{1,0:T(8,128)(2,1)} %get-tuple-element.468.a_ref), channel_id=1, source_target_pairs={{0,1},{3,2},{4,5},{7,6},{8,9},{11,10},{12,13},{15,14},{16,17},{19,... | collective-permute-start | bytes 1769480 | tf_op jit(solution)/shard_map/ppermute | solution.py:531
  353.5 17.7 %collective-permute-start.41 = (bf16[256,1152]{1,0:T(8,128)(2,1)}, bf16[256,1152]{1,0:T(8,128)(2,1)}, u32[]{:S(2)}, u32[]{:S(2)}) collective-permute-start(bf16[256,1152]{1,0:T(8,128)(2,1)} %copy-done.47), channel_id=1, source_target_pairs={{1,2},{2,1},{5,6},{6,5},{9,10},{10,9},{13,14},{14,13},{17,18},{18,... | collective-permute-start | bytes 1769480 | tf_op jit(solution)/shard_map/ppermute | solution.py:531
  355.2 18.7 %collective-permute-start.40 = (bf16[256,1152]{1,0:T(8,128)(2,1)S(1)}, bf16[256,1152]{1,0:T(8,128)(2,1)}, u32[]{:S(2)}, u32[]{:S(2)}) collective-permute-start(bf16[256,1152]{1,0:T(8,128)(2,1)S(1)} %add.147.refs_1_), channel_id=1, source_target_pairs={{1,0},{2,3},{5,4},{6,7},{9,8},{10,11},{13,12},{14,15},{17,16},{18,... | collective-permute-start | bytes 1769480 | tf_op jit(solution)/shard_map/ppermute | solution.py:531
  369.2 16.9 %collective-permute-start.45 = (bf16[256,1152]{1,0:T(8,128)(2,1)S(1)}, bf16[256,1152]{1,0:T(8,128)(2,1)S(1)}, u32[]{:S(2)}, u32[]{:S(2)}) collective-permute-start(bf16[256,1152]{1,0:T(8,128)(2,1)S(1)} %add.148.a_ref), channel_id=1, source_target_pairs={{1,2},{2,1},{5,6},{6,5},{9,10},{10,9},{13,14},{14,13},{17,18},{18,... | collective-permute-start | bytes 1769480 | tf_op jit(solution)/shard_map/ppermute | solution.py:531
  372.4 21.1 %collective-permute-start.44 = (bf16[256,1152]{1,0:T(8,128)(2,1)S(1)}, bf16[256,1152]{1,0:T(8,128)(2,1)S(1)}, u32[]{:S(2)}, u32[]{:S(2)}) collective-permute-start(bf16[256,1152]{1,0:T(8,128)(2,1)S(1)} %add.149.refs_1_), channel_id=1, source_target_pairs={{1,0},{2,3},{5,4},{6,7},{9,8},{10,11},{13,12},{14,15},{17,16},{18,... | collective-permute-start | bytes 1769480 | tf_op jit(solution)/shard_map/ppermute | solution.py:531
  385.4 9.8 %collective-permute-start.43 = (bf16[256,1152]{1,0:T(8,128)(2,1)S(1)}, bf16[256,1152]{1,0:T(8,128)(2,1)S(1)}, u32[]{:S(2)}, u32[]{:S(2)}) collective-permute-start(bf16[256,1152]{1,0:T(8,128)(2,1)S(1)} %add.150.a_ref), channel_id=1, source_target_pairs={{1,2},{2,1},{5,6},{6,5},{9,10},{10,9},{13,14},{14,13},{17,18},{18,... | collective-permute-start | bytes 1769480 | tf_op jit(solution)/shard_map/ppermute | solution.py:531
  386.3 46.7 %collective-permute-start.47 = (bf16[256,1152]{1,0:T(8,128)(2,1)S(1)}, bf16[256,1152]{1,0:T(8,128)(2,1)}, u32[]{:S(2)}, u32[]{:S(2)}) collective-permute-start(bf16[256,1152]{1,0:T(8,128)(2,1)S(1)} %add.151.refs_1_), channel_id=1, source_target_pairs={{1,0},{2,3},{5,4},{6,7},{9,8},{10,11},{13,12},{14,15},{17,16},{18,... | collective-permute-start | bytes 1769480 | tf_op jit(solution)/shard_map/ppermute | solution.py:531
  396.2 41.9 %collective-permute-start.46 = (bf16[256,1152]{1,0:T(8,128)(2,1)}, bf16[256,1152]{1,0:T(8,128)(2,1)}, u32[]{:S(2)}, u32[]{:S(2)}) collective-permute-start(bf16[256,1152]{1,0:T(8,128)(2,1)} %add.152.refs_1_), channel_id=1, source_target_pairs={{1,0},{2,3},{5,4},{6,7},{9,8},{10,11},{13,12},{14,15},{17,16},{18,... | collective-permute-start | bytes 1769480 | tf_op jit(solution)/shard_map/ppermute | solution.py:531
  (73 other events, 540.7 us)
Sparse Core Ops, SparseCore 0:
  213.2 94.2 all-reduce.7
  352.5 66.6 all-reduce.5
